TPU v7x, 128 devices: a whole 4x4x4 slice. The times are simulated.
128 devices in a mesh: lat: 8 (over x, core), lon: 16 (over z, y).
Axes of the slice: x: 4, y: 4, z: 4, core: 2. Of those that a mesh axis runs over, the one named last changes fastest.
Arguments:
- fields: bfloat16 [256, 2048, 128], P('lat', 'lon'), may hold values from -6 to 6
- cotangent: bfloat16 [256, 2048, 128], P('lat', 'lon'), may hold values from -6 to 6
- kernel_bank: bfloat16 [256, 9, 128, 128], P(('lat', 'lon')), may hold values from -0.1875 to 0.1875
- block_expert: int32 [16, 128], P('lat', 'lon'), may hold values from 0 to 255, as said below
- owner: int32 [256], replicated, may hold values from 0 to 255, as said below
Outputs:
- outputs: bfloat16 [256, 2048, 128], P('lat', 'lon')
- grad_fields: bfloat16 [256, 2048, 128], P('lat', 'lon')
- grad_bank: float32 [256, 9, 128, 128], P(('lat', 'lon'))
Inputs may be any that keep to these rules, and one draw needn't show every extreme that they name: owner is a permutation: each expert is stored in exactly one row of kernel_bank. `block_expert`: call the lon column of expert e the value (owner[e] // 2) modulo the number of devices along lon. Among the 2 x 8 blocks of one device, at most 2 name experts of any one lon column; in every latitude band of devices one column is named by exactly 2 blocks of each device of that band.
All inputs are finite; a program needn't handle non-finite values.
Results may differ from a plain program's by a relative error of at most 0.0032.
Values may be sent and summed in bfloat16 or wider, within the bound.
A program may use at most 192 MiB of HBM per device.

v0:
```python
import jax
import jax.numpy as jnp
from jax import lax
from jax.experimental import pallas as pl
from jax.experimental.pallas import tpu as pltpu
from jax.sharding import PartitionSpec as P

BS = 16
CAP = 2
C = 128
NLAT = 8
NLON = 16
RING = 4
BLK = 16
BLON = 8
HEIGHT = 32
WIDTH = 128
ROWS = BS + 2
TILES = ROWS + 4
EXT_ROWS = HEIGHT + 2
EXT_COLS = WIDTH + 2 * BS
MESH = pl.DeviceIdType.MESH
F32 = jnp.float32
BF16 = jnp.bfloat16


def peer_lon(me, k):
    z, y = me // RING, lax.rem(me, RING)
    return lax.rem(z + k // RING, RING) * RING + lax.rem(y + lax.rem(k, RING), RING)


def source_lon(me, k):
    z, y = me // RING, lax.rem(me, RING)
    return lax.rem(z + RING - k // RING, RING) * RING + lax.rem(y + RING - lax.rem(k, RING), RING)


def greet(lat, lon, diagonal):
    barrier = pltpu.get_barrier_semaphore()

    def signal(device):
        pl.semaphore_signal(barrier, inc=1, device_id=device, device_id_type=MESH)

    @pl.loop(1, NLON)
    def _(k):
        signal((lat, peer_lon(lon, k)))

    @pl.loop(1, NLAT)
    def _(k):
        signal((lax.rem(lat + k, NLAT), lon))

    for up, side in diagonal:
        signal((lax.rem(lat + up, NLAT), lax.rem(lon + side, NLON)))
    pl.semaphore_wait(barrier, NLON - 1 + NLAT - 1 + len(diagonal))


DIAGONAL = ((NLAT - 1, NLON - 1), (NLAT - 1, 1), (1, NLON - 1), (1, 1))


def index_tables(expert_ref, owner_ref, column, local, slot_block):
    for b in range(BLK):
        stored = owner_ref[expert_ref[b // BLON, b % BLON]]
        group = stored >> 1
        column[b] = group & (NLON - 1)
        local[b] = (group >> 4) * 2 + (stored & 1)

    @pl.loop(0, NLON)
    def _(c):
        first = jnp.int32(-1)
        second = jnp.int32(-1)
        for b in range(BLK):
            here = column[b] == c
            second = jnp.where(here & (first >= 0), b, second)
            first = jnp.where(here & (first < 0), b, first)
        slot_block[2 * c] = first
        slot_block[2 * c + 1] = second


def send_kernel(
    expert_ref, owner_ref, fields, cot, bank,
    patch_out, cot_out, id_out, kern_out,
    column, local, slot_block, ext, wide, side_l, side_r, cot_in, patch_in, cot_stage, patch_stage, id_stage,
    load_sem, halo_send, halo_recv, bank_send, bank_recv, cot_send, cot_recv,
    patch_send, patch_recv, id_send, id_recv,
):
    lat, lon = lax.axis_index("lat"), lax.axis_index("lon")
    load_fields = pltpu.make_async_copy(
        fields, ext.at[pl.ds(1, HEIGHT), pl.ds(BS, WIDTH)], load_sem.at[0]
    )
    load_fields.start()

    def load_cot(b):
        rows = pl.ds(pl.multiple_of((b // BLON) * BS, BS), BS)
        cols = pl.ds(pl.multiple_of(lax.rem(b, BLON) * BS, BS), BS)
        return pltpu.make_async_copy(cot.at[rows, cols], cot_in.at[b], load_sem.at[6 + b])

    @pl.loop(0, BLK)
    def _(b):
        load_cot(b).start()

    own_bank = pltpu.make_async_copy(bank, kern_out.at[lat], load_sem.at[2])
    own_bank.start()
    index_tables(expert_ref, owner_ref, column, local, slot_block)
    greet(lat, lon, DIAGONAL)

    up, down = lax.rem(lat + NLAT - 1, NLAT), lax.rem(lat + 1, NLAT)
    left, right = lax.rem(lon + NLON - 1, NLON), lax.rem(lon + 1, NLON)
    top, bottom = pl.ds(0, 1), pl.ds(HEIGHT - 1, 1)
    first, last = pl.ds(0, BS), pl.ds(WIDTH - BS, BS)
    all_rows, all_cols = pl.ds(0, HEIGHT), pl.ds(0, WIDTH)
    mid_rows, mid_cols = pl.ds(1, HEIGHT), pl.ds(BS, WIDTH)
    low, high = pl.ds(0, BS), pl.ds(BS + WIDTH, BS)
    zero, end = pl.ds(0, 1), pl.ds(EXT_ROWS - 1, 1)
    moves = (
        (top, all_cols, end, mid_cols, (up, lon)),
        (bottom, all_cols, zero, mid_cols, (down, lon)),
        (all_rows, first, mid_rows, high, (lat, left)),
        (all_rows, last, mid_rows, low, (lat, right)),
        (top, first, end, high, (up, left)),
        (top, last, end, low, (up, right)),
        (bottom, first, zero, high, (down, left)),
        (bottom, last, zero, low, (down, right)),
    )
    halos = []
    for i, (rows, cols, to_rows, to_cols, device) in enumerate(moves):
        copy = pltpu.make_async_remote_copy(
            fields.at[rows, cols], ext.at[to_rows, to_cols], halo_send.at[i], halo_recv.at[i],
            device_id=device, device_id_type=MESH,
        )
        copy.start()
        halos.append(copy)

    def cot_copy(k, r):
        dst = peer_lon(lon, k)
        return pltpu.make_async_remote_copy(
            cot_stage.at[dst, r], cot_out.at[lon, r], cot_send.at[r, k], cot_recv.at[r, k],
            device_id=(lat, dst), device_id_type=MESH,
        )

    def id_copy(k):
        dst = peer_lon(lon, k)
        return pltpu.make_async_remote_copy(
            id_stage.at[dst], id_out.at[lon], id_send.at[k], id_recv.at[k],
            device_id=(lat, dst), device_id_type=MESH,
        )

    def patch_copy(k, r):
        dst = peer_lon(lon, k)
        return pltpu.make_async_remote_copy(
            patch_stage.at[dst, r], patch_out.at[lon, r], patch_send.at[r, k], patch_recv.at[r, k],
            device_id=(lat, dst), device_id_type=MESH,
        )

    def bank_copy(k):
        return pltpu.make_async_remote_copy(
            bank, kern_out.at[lat], bank_send.at[k], bank_recv.at[k],
            device_id=(lax.rem(lat + k, NLAT), lon), device_id_type=MESH,
        )

    lane = lax.broadcasted_iota(jnp.int32, (1, C), 1)

    @pl.loop(0, BLK)
    def _(b):
        load_cot(b).wait()

    def stage_cot(k, r):
        dst = peer_lon(lon, k)
        cot_stage[dst, r] = cot_in[jnp.maximum(slot_block[2 * dst + r], 0)]

    @pl.loop(1, NLON)
    def _(k):
        stage_cot(k, 0)
        cot_copy(k, 0).start()

    @pl.loop(1, NLAT)
    def _(k):
        bank_copy(k).start()

    @pl.loop(1, NLON)
    def _(k):
        stage_cot(k, 1)
        cot_copy(k, 1).start()

    @pl.loop(0, NLON)
    def _(c):
        ids = []
        for r in range(CAP):
            found = slot_block[2 * c + r]
            ids.append(jnp.where(found < 0, -1, local[jnp.maximum(found, 0)]))
        id_stage[c] = jnp.where(lane == 0, ids[0], ids[1])

    @pl.loop(1, NLON)
    def _(k):
        id_copy(k).start()

    stage_cot(0, 0)
    stage_cot(0, 1)
    own_cot = pltpu.make_async_copy(cot_stage.at[lon], cot_out.at[lon], load_sem.at[3])
    own_ids = pltpu.make_async_copy(id_stage.at[lon], id_out.at[lon], load_sem.at[4])
    own_cot.start()
    own_ids.start()

    load_fields.wait()
    for copy in halos:
        copy.wait()

    @pl.when(lat == 0)
    def _():
        ext[0] = jnp.zeros((EXT_COLS, C), BF16)

    @pl.when(lat == NLAT - 1)
    def _():
        ext[EXT_ROWS - 1] = jnp.zeros((EXT_COLS, C), BF16)

    @pl.loop(0, EXT_ROWS)
    def _(r):
        wide[pl.ds(pl.multiple_of(r * EXT_COLS, BS), EXT_COLS), :] = ext[r].astype(F32)

    @pl.loop(0, BLON)
    def _(k):
        side_l[k, pl.ds(0, EXT_ROWS)] = wide[
            pl.ds(k * BS + BS - 1, EXT_ROWS, stride=EXT_COLS), :
        ].astype(BF16)
        side_r[k, pl.ds(0, EXT_ROWS)] = wide[
            pl.ds(k * BS + 2 * BS, EXT_ROWS, stride=EXT_COLS), :
        ].astype(BF16)

    @pl.loop(0, BLK)
    def _(b):
        row = pl.multiple_of((b // BLON) * BS, BS)
        col = lax.rem(b, BLON)
        patch_in[b, pl.ds(0, ROWS)] = ext[
            pl.ds(row, ROWS), pl.ds(pl.multiple_of((col + 1) * BS, BS), BS), :
        ]
        patch_in[b, pl.ds(ROWS, 2)] = side_l[col, pl.ds(row, 2 * BS)].reshape(2, BS, C)
        patch_in[b, pl.ds(ROWS + 2, 2)] = side_r[col, pl.ds(row, 2 * BS)].reshape(2, BS, C)

    def stage_patch(k, r):
        dst = peer_lon(lon, k)
        patch_stage[dst, r] = patch_in[jnp.maximum(slot_block[2 * dst + r], 0)]

    for r in range(CAP):
        @pl.loop(1, NLON)
        def _(k):
            stage_patch(k, r)
            patch_copy(k, r).start()

    stage_patch(0, 0)
    stage_patch(0, 1)
    own_patch = pltpu.make_async_copy(patch_stage.at[lon], patch_out.at[lon], load_sem.at[5])
    own_patch.start()
    own_bank.wait()
    own_cot.wait()
    own_ids.wait()
    own_patch.wait()

    @pl.loop(1, NLAT)
    def _(k):
        bank_copy(k).wait()

    @pl.loop(1, NLON)
    def _(k):
        id_copy(k).wait()
        for r in range(CAP):
            cot_copy(k, r).wait()
            patch_copy(k, r).wait()


def send_blocks(block_expert, owner, fields, cotangent, bank):
    hbm = pl.BlockSpec(memory_space=pltpu.HBM)
    smem = pl.BlockSpec(memory_space=pltpu.SMEM)
    dma = pltpu.SemaphoreType.DMA
    return pl.pallas_call(
        send_kernel,
        out_shape=(
            jax.ShapeDtypeStruct((NLON, CAP, TILES, BS, C), BF16),
            jax.ShapeDtypeStruct((NLON, CAP, BS, BS, C), BF16),
            jax.ShapeDtypeStruct((NLON, 1, C), jnp.int32),
            jax.ShapeDtypeStruct((NLAT,) + bank.shape, BF16),
        ),
        in_specs=[smem, smem, hbm, hbm, hbm],
        out_specs=(hbm, hbm, hbm, hbm),
        scratch_shapes=[
            pltpu.SMEM((BLK,), jnp.int32),
            pltpu.SMEM((BLK,), jnp.int32),
            pltpu.SMEM((NLON * CAP,), jnp.int32),
            pltpu.VMEM((EXT_ROWS, EXT_COLS, C), BF16),
            pltpu.VMEM((EXT_ROWS * EXT_COLS, C), F32),
            pltpu.VMEM((BLON, 3 * BS, C), BF16),
            pltpu.VMEM((BLON, 3 * BS, C), BF16),
            pltpu.VMEM((BLK, BS, BS, C), BF16),
            pltpu.VMEM((BLK, TILES, BS, C), BF16),
            pltpu.VMEM((NLON, CAP, BS, BS, C), BF16),
            pltpu.VMEM((NLON, CAP, TILES, BS, C), BF16),
            pltpu.VMEM((NLON, 1, C), jnp.int32),
            dma((6 + BLK,)),
            dma((8,)), dma((8,)),
            dma((NLAT,)), dma((NLAT,)),
            dma((CAP, NLON)), dma((CAP, NLON)),
            dma((CAP, NLON)), dma((CAP, NLON)),
            dma((NLON,)), dma((NLON,)),
        ],
        compiler_params=pltpu.CompilerParams(
            collective_id=0, has_side_effects=True, vmem_limit_bytes=40 << 20
        ),
    )(block_expert, owner, fields, cotangent, bank)


def compute_kernel(
    ids, patch, cot, kern, out, spread, grads,
    pad, taps, wide_cot, shift, total, started,
):
    step = pl.program_id(0)

    @pl.when(step == 0)
    def _():
        wide_cot[...] = jnp.zeros_like(wide_cot)
        for e in range(NLON):
            started[e] = 0

    for r in range(CAP):
        found = ids[step, 0, r]

        @pl.when(found >= 0)
        def _():
            e = jnp.maximum(found, 0)
            pad[:, pl.ds(8, BS), :] = patch[0, r, pl.ds(0, ROWS)].astype(F32)
            left = patch[0, r, pl.ds(ROWS, 2)].reshape(2 * BS, C)[:ROWS].astype(F32)
            right = patch[0, r, pl.ds(ROWS + 2, 2)].reshape(2 * BS, C)[:ROWS].astype(F32)
            pad[:, 7, :] = left
            pad[:, BS + 8, :] = right
            for b in range(3):
                taps[:, pl.ds(b * C, C)] = pad[:, pl.ds(7 + b, BS), :].reshape(ROWS * BS, C).astype(BF16)
            cots = cot[0, r].reshape(BS * BS, C)
            for a in range(3):
                wide_cot[pl.ds(a * BS, BS * BS), pl.ds(a * C, C)] = cots
            weights = [kern[e, pl.ds(3 * a, 3)].reshape(3 * C, C) for a in range(3)]
            result = jnp.zeros((BS * BS, C), F32)
            for a in range(3):
                result += jnp.dot(
                    taps[pl.ds(a * BS, BS * BS), :], weights[a], preferred_element_type=F32
                )
            out[0, r] = result.astype(BF16).reshape(BS, BS, C)
            both = jnp.concatenate(weights, axis=1)
            grid = lax.dot_general(
                wide_cot[...], both, (((1,), (1,)), ((), ())), preferred_element_type=F32
            )
            shift[0, :, pl.ds(8, BS), :] = grid[:, :C].reshape(ROWS, BS, C)
            shift[1, :, pl.ds(8, BS), :] = grid[:, 2 * C:].reshape(ROWS, BS, C)
            place = lax.broadcasted_iota(jnp.int32, (ROWS, BS, C), 1)
            main = grid[:, C:2 * C].reshape(ROWS, BS, C)
            main += jnp.where(place == BS - 1, 0.0, shift[0, :, pl.ds(9, BS), :])
            main += jnp.where(place == 0, 0.0, shift[1, :, pl.ds(7, BS), :])
            spread[0, r, pl.ds(0, ROWS)] = main.astype(BF16)
            tail = jnp.zeros((2 * BS - ROWS, C), F32)
            lefts = jnp.concatenate([shift[0, :, 8, :], tail], axis=0)
            rights = jnp.concatenate([shift[1, :, BS + 7, :], tail], axis=0)
            spread[0, r, pl.ds(ROWS, 2)] = lefts.astype(BF16).reshape(2, BS, C)
            spread[0, r, pl.ds(ROWS + 2, 2)] = rights.astype(BF16).reshape(2, BS, C)
            keep = started[e] > 0
            for a in range(3):
                term = lax.dot_general(
                    taps[pl.ds(a * BS, BS * BS), :], cots, (((0,), (0,)), ((), ())),
                    preferred_element_type=F32,
                ).reshape(3, C, C)
                before = total[e, pl.ds(3 * a, 3)]
                total[e, pl.ds(3 * a, 3)] = jnp.where(keep, before, 0.0) + term
            started[e] = 1

    @pl.when(step == NLON - 1)
    def _():
        @pl.loop(0, NLON)
        def _(e):
            grads[e] = jnp.where(started[e] > 0, total[e], 0.0).astype(BF16)


def compute(ids, patches, cots, kernels):
    slot = lambda rows: pl.BlockSpec((1, CAP, rows, BS, C), lambda s: (s, 0, 0, 0, 0))
    whole = pl.BlockSpec((NLON, 9, C, C), lambda s: (0, 0, 0, 0), pipeline_mode=pl.Buffered(1))
    return pl.pallas_call(
        compute_kernel,
        grid=(NLON,),
        out_shape=(
            jax.ShapeDtypeStruct((NLON, CAP, BS, BS, C), BF16),
            jax.ShapeDtypeStruct((NLON, CAP, TILES, BS, C), BF16),
            jax.ShapeDtypeStruct((NLON, 9, C, C), BF16),
        ),
        in_specs=[pl.BlockSpec(memory_space=pltpu.SMEM), slot(TILES), slot(BS), whole],
        out_specs=(slot(BS), slot(TILES), whole),
        scratch_shapes=[
            pltpu.VMEM((ROWS, 2 * BS, C), F32),
            pltpu.VMEM((ROWS * BS, 3 * C), BF16),
            pltpu.VMEM((ROWS * BS, 3 * C), BF16),
            pltpu.VMEM((2, ROWS, 2 * BS, C), F32),
            pltpu.VMEM((NLON, 9, C, C), F32),
            pltpu.SMEM((NLON,), jnp.int32),
        ],
        compiler_params=pltpu.CompilerParams(vmem_limit_bytes=48 << 20),
    )(ids, patches, cots, kernels)


def return_kernel(
    expert_ref, owner_ref, blocks, spreads, grads,
    outputs, result, bank_out,
    column, local, slot_block, block_slot, got_out, got_spread, got_grads, canvas, block,
    row_in, col_in, corner_in,
    load_sem, grad_send, grad_recv, out_send, out_recv, spread_send, spread_recv, halo_send, halo_recv,
):
    lat, lon = lax.axis_index("lat"), lax.axis_index("lon")
    own = [
        pltpu.make_async_copy(blocks.at[lon], got_out.at[pl.ds(2 * lon, CAP)], load_sem.at[0]),
        pltpu.make_async_copy(spreads.at[lon], got_spread.at[pl.ds(2 * lon, CAP)], load_sem.at[1]),
        pltpu.make_async_copy(grads.at[lat], got_grads.at[lat], load_sem.at[2]),
    ]
    for copy in own:
        copy.start()
    greet(lat, lon, DIAGONAL)

    def spread_copy(k, r):
        dst = peer_lon(lon, k)
        return pltpu.make_async_remote_copy(
            spreads.at[dst, r], got_spread.at[2 * lon + r], spread_send.at[r, k], spread_recv.at[r, k],
            device_id=(lat, dst), device_id_type=MESH,
        )

    def out_copy(k, r):
        dst = peer_lon(lon, k)
        return pltpu.make_async_remote_copy(
            blocks.at[dst, r], got_out.at[2 * lon + r], out_send.at[r, k], out_recv.at[r, k],
            device_id=(lat, dst), device_id_type=MESH,
        )

    def grad_copy(k):
        dst = lax.rem(lat + k, NLAT)
        return pltpu.make_async_remote_copy(
            grads.at[dst], got_grads.at[lat], grad_send.at[k], grad_recv.at[k],
            device_id=(dst, lon), device_id_type=MESH,
        )

    @pl.loop(1, NLON)
    def _(k):
        spread_copy(k, 0).start()

    @pl.loop(1, NLAT)
    def _(k):
        grad_copy(k).start()

    @pl.loop(1, NLON)
    def _(k):
        spread_copy(k, 1).start()

    for r in range(CAP):
        @pl.loop(1, NLON)
        def _(k):
            out_copy(k, r).start()

    index_tables(expert_ref, owner_ref, column, local, slot_block)
    for b in range(BLK):
        c = column[b]
        block_slot[b] = 2 * c + jnp.where(slot_block[2 * c + 1] == b, 1, 0)
    canvas[...] = jnp.zeros_like(canvas)

    @pl.loop(1, NLON)
    def _(k):
        for r in range(CAP):
            spread_copy(k, r).wait()

    for copy in own:
        copy.wait()

    @pl.loop(0, BLK)
    def _(b):
        bi, bj = b // BLON, lax.rem(b, BLON)
        slot = block_slot[b]
        base = bi * BS * EXT_COLS + (bj + 1) * BS
        block[...] = got_spread[slot]

        @pl.loop(0, ROWS)
        def _(i):
            at = pl.ds(pl.multiple_of(base + i * EXT_COLS, BS), BS)
            canvas[at, :] += block[i].astype(F32)

        lefts = block[pl.ds(ROWS, 2)].reshape(2 * BS, C)[:ROWS].astype(F32)
        rights = block[pl.ds(ROWS + 2, 2)].reshape(2 * BS, C)[:ROWS].astype(F32)
        canvas[pl.ds(base - 1, ROWS, stride=EXT_COLS), :] += lefts
        canvas[pl.ds(base + BS, ROWS, stride=EXT_COLS), :] += rights

    up, down = lax.rem(lat + NLAT - 1, NLAT), lax.rem(lat + 1, NLAT)
    left, right = lax.rem(lon + NLON - 1, NLON), lax.rem(lon + 1, NLON)
    grid = canvas.reshape(EXT_ROWS, EXT_COLS, C)
    half = BS // 2
    low, high = pl.ds(half, half), pl.ds(BS + WIDTH, half)
    cols, rows = pl.ds(BS, WIDTH), pl.ds(1, HEIGHT)
    moves = (
        (grid.at[0, cols], row_in.at[0], (up, lon)),
        (grid.at[EXT_ROWS - 1, cols], row_in.at[1], (down, lon)),
        (grid.at[rows, low], col_in.at[0], (lat, left)),
        (grid.at[rows, high], col_in.at[1], (lat, right)),
        (grid.at[0, low], corner_in.at[0], (up, left)),
        (grid.at[0, high], corner_in.at[1], (up, right)),
        (grid.at[EXT_ROWS - 1, low], corner_in.at[2], (down, left)),
        (grid.at[EXT_ROWS - 1, high], corner_in.at[3], (down, right)),
    )
    halos = []
    for i, (source, target, device) in enumerate(moves):
        copy = pltpu.make_async_remote_copy(
            source, target, halo_send.at[i], halo_recv.at[i],
            device_id=device, device_id_type=MESH,
        )
        copy.start()
        halos.append(copy)

    @pl.loop(1, NLAT)
    def _(k):
        grad_copy(k).wait()

    for e in range(2):
        @pl.loop(0, 9)
        def _(t):
            sums = got_grads[0, e, t].astype(F32)
            for i in range(1, NLAT):
                sums += got_grads[i, e, t].astype(F32)
            bank_out[e, t] = sums

    @pl.loop(1, NLON)
    def _(k):
        for r in range(CAP):
            out_copy(k, r).wait()

    @pl.loop(0, BLK)
    def _(b):
        bi, bj = b // BLON, lax.rem(b, BLON)
        slot = block_slot[b]
        outputs[
            pl.ds(pl.multiple_of(bi * BS, BS), BS), pl.ds(pl.multiple_of(bj * BS, BS), BS), :
        ] = got_out[slot]

    for copy in halos:
        copy.wait()
    from_down = jnp.where(lat < NLAT - 1, 1.0, 0.0).astype(F32)
    from_up = jnp.where(lat > 0, 1.0, 0.0).astype(F32)
    top, bottom = EXT_COLS, HEIGHT * EXT_COLS
    canvas[pl.ds(bottom + BS, WIDTH), :] += row_in[0] * from_down
    canvas[pl.ds(top + BS, WIDTH), :] += row_in[1] * from_up
    near, far = pl.ds(BS, half), pl.ds(BS + WIDTH - half, half)

    @pl.loop(0, HEIGHT)
    def _(i):
        start = pl.multiple_of((i + 1) * EXT_COLS, BS)
        canvas[pl.ds(start + BS + WIDTH - half, half), :] += col_in[0, i]
        canvas[pl.ds(start + BS, half), :] += col_in[1, i]

    canvas[pl.ds(bottom + BS + WIDTH - half, half), :] += corner_in[0] * from_down
    canvas[pl.ds(bottom + BS, half), :] += corner_in[1] * from_down
    canvas[pl.ds(top + BS + WIDTH - half, half), :] += corner_in[2] * from_up
    canvas[pl.ds(top + BS, half), :] += corner_in[3] * from_up

    @pl.loop(0, HEIGHT)
    def _(i):
        start = pl.multiple_of((i + 1) * EXT_COLS + BS, BS)
        result[i] = canvas[pl.ds(start, WIDTH), :].astype(BF16)


def return_blocks(block_expert, owner, blocks, spreads, grads):
    hbm = pl.BlockSpec(memory_space=pltpu.HBM)
    smem = pl.BlockSpec(memory_space=pltpu.SMEM)
    vmem = pl.BlockSpec(memory_space=pltpu.VMEM)
    dma = pltpu.SemaphoreType.DMA
    return pl.pallas_call(
        return_kernel,
        out_shape=(
            jax.ShapeDtypeStruct((HEIGHT, WIDTH, C), BF16),
            jax.ShapeDtypeStruct((HEIGHT, WIDTH, C), BF16),
            jax.ShapeDtypeStruct((2, 9, C, C), F32),
        ),
        in_specs=[smem, smem, hbm, hbm, hbm],
        out_specs=(vmem, vmem, vmem),
        scratch_shapes=[
            pltpu.SMEM((BLK,), jnp.int32),
            pltpu.SMEM((BLK,), jnp.int32),
            pltpu.SMEM((NLON * CAP,), jnp.int32),
            pltpu.SMEM((BLK,), jnp.int32),
            pltpu.VMEM((NLON * CAP, BS, BS, C), BF16),
            pltpu.VMEM((NLON * CAP, TILES, BS, C), BF16),
            pltpu.VMEM((NLAT, 2, 9, C, C), BF16),
            pltpu.VMEM((EXT_ROWS * EXT_COLS, C), F32),
            pltpu.VMEM((TILES, BS, C), BF16),
            pltpu.VMEM((2, WIDTH, C), F32),
            pltpu.VMEM((2, HEIGHT, BS // 2, C), F32),
            pltpu.VMEM((4, BS // 2, C), F32),
            dma((3,)),
            dma((NLAT,)), dma((NLAT,)),
            dma((CAP, NLON)), dma((CAP, NLON)),
            dma((CAP, NLON)), dma((CAP, NLON)),
            dma((8,)), dma((8,)),
        ],
        compiler_params=pltpu.CompilerParams(
            collective_id=1, has_side_effects=True, vmem_limit_bytes=48 << 20
        ),
    )(block_expert, owner, blocks, spreads, grads)


def local(fields, cotangent, kernel_bank, block_expert, owner):
    patches, cots, ids, kernels = send_blocks(block_expert, owner, fields, cotangent, kernel_bank)
    blocks, spreads, grads = compute(ids, patches, cots, kernels.reshape(NLON, 9, C, C))
    return return_blocks(block_expert, owner, blocks, spreads, grads.reshape(NLAT, 2, 9, C, C))


def solution(mesh):
    return jax.shard_map(
        local,
        mesh=mesh,
        in_specs=(
            P("lat", "lon", None),
            P("lat", "lon", None),
            P(("lat", "lon"), None, None, None),
            P("lat", "lon"),
            P(),
        ),
        out_specs=(
            P("lat", "lon", None),
            P("lat", "lon", None),
            P(("lat", "lon"), None, None, None),
        ),
        check_vma=False,
    )
```

profile of v0, /device:TPU:1, one launch (start us, length us, event | category | flops | bytes accessed | tf_op | source)
XLA Modules:
  0.0 187.4 jit_solution(6811597785551751279)
XLA Ops:
  0.6 0.0 copy-start.2
  0.6 1.2 copy-done.2
  1.9 0.0 copy-start.3
  1.9 1.2 copy-done.3
  3.1 0.0 copy-start.4
  3.1 1.1 copy-done.4
  4.1 0.0 copy-start.5
  4.1 0.7 copy-done.5
  4.8 0.0 copy-start.7
  4.8 0.7 copy-done.7
  5.5 75.3 %shard_map.76 = (bf16[16,2,22,16,128]{4,3,2,1,0:T(8,128)(2,1)S(1)}, bf16[16,2,16,16,128]{4,3,2,1,0:T(8,128)(2,1)S(1)}, s32[16,1,128]{2,1,0:T(1,128)S(1)}, bf16[8,2,9,128,128]{4,3,2,1,0:T(8,128)(2,1)S(1)}) custom-call(s32[2,8]{1,0:T(2,128)S(1)} %copy-done.5, s32[256]{0:T(256)S(1)} %copy-done.7, bf16[32,128,128]{2,1,0:T(8,128)(2,1)S(1)} %copy-done.2, ...), custom_call_target="tpu_custom_call" | custom-call | tf_op jit(solution)/shard_map/pallas_call | solution.py:272
  80.8 0.0 copy-start
  80.8 2.1 %copy-done = bf16[8,2,9,128,128]{4,3,2,1,0:T(8,128)(2,1)} copy-done((bf16[8,2,9,128,128]{4,3,2,1,0:T(8,128)(2,1)}, bf16[8,2,9,128,128]{4,3,2,1,0:T(8,128)(2,1)S(1)}, u32[]{:S(2)}) %copy-start) | copy-done | bytes 4718616
  83.0 0.0 copy-start.1
  83.0 1.5 copy-done.1
  84.5 0.0 copy-start.6
  84.5 0.0 copy-start.8
  84.5 20.6 %shard_map.77 = (bf16[16,2,16,16,128]{4,3,2,1,0:T(8,128)(2,1)S(1)}, bf16[16,2,22,16,128]{4,3,2,1,0:T(8,128)(2,1)}, bf16[16,9,128,128]{3,2,1,0:T(8,128)(2,1)}) custom-call(s32[16,1,128]{2,1,0:T(1,128)S(1)} %get-tuple-element.10.ids, bf16[16,2,22,16,128]{4,3,2,1,0:T(8,128)(2,1)} %copy-done.1, bf16[16,2,16,16,128]{4,3,2,1,0:T(8,128)(2,1)S(1)} %get-tuple-element.12.cot, ...), custom_call_target="tpu_custom_call" | custom-call | tf_op jit(solution)/shard_map/pallas_call | solution.py:379
  105.1 0.0 copy-done.6
  105.1 0.0 copy-done.8
  105.1 79.3 %shard_map.78 = (bf16[32,128,128]{2,1,0:T(8,128)(2,1)S(1)}, bf16[32,128,128]{2,1,0:T(8,128)(2,1)S(1)}, f32[2,9,128,128]{3,2,1,0:T(8,128)S(1)}) custom-call(s32[2,8]{1,0:T(2,128)S(1)} %copy-done.6, s32[256]{0:T(256)S(1)} %copy-done.8, bf16[16,2,16,16,128]{4,3,2,1,0:T(8,128)(2,1)S(1)} %get-tuple-element.14.blocks, ...), custom_call_target="tpu_custom_call" | custom-call | tf_op jit(solution)/shard_map/pallas_call | solution.py:568
  184.5 1.0 copy.11
  185.5 1.0 copy.12
  186.4 1.0 copy.13
Async XLA Ops:
  0.6 1.2 copy-start.2
  1.9 1.2 copy-start.3
  3.1 1.1 copy-start.4
  4.1 0.7 copy-start.5
  4.8 0.7 copy-start.7
  80.8 2.1 %copy-start = (bf16[8,2,9,128,128]{4,3,2,1,0:T(8,128)(2,1)}, bf16[8,2,9,128,128]{4,3,2,1,0:T(8,128)(2,1)S(1)}, u32[]{:S(2)}) copy-start(bf16[8,2,9,128,128]{4,3,2,1,0:T(8,128)(2,1)S(1)} %get-tuple-element.13) | copy-start | bytes 14155780
  83.0 1.5 copy-start.1
  84.5 20.6 %copy-start.6 = (s32[2,8]{1,0:T(2,128)S(1)}, s32[2,8]{1,0:T(2,128)}, u32[]{:S(2)}) copy-start(s32[2,8]{1,0:T(2,128)} %expert_ref.3) | copy-start | bytes 196
  84.5 20.6 %copy-start.8 = (s32[256]{0:T(256)S(1)}, s32[256]{0:T(256)}, u32[]{:S(2)}) copy-start(s32[256]{0:T(256)} %owner_ref.3) | copy-start | bytes 3076
where the time goes:
time: 188 us; the launch traced here: 187 us
  Pallas kernels  175 us (93%)
  local copies, waits for them, and re-layouts  11.5 us (6%)
    pallas_call x1, Pallas kernels, return_blocks(): pl.pallas_call(return_kernel, out_shape=(jax.ShapeDtypeStruct((HEIGHT, WI...  79.3 us
    pallas_call x1, Pallas kernels, send_blocks(): pl.pallas_call(send_kernel, out_shape=(jax.ShapeDtypeStruct((NLON, CAP, T...  75.3 us
    pallas_call x1, Pallas kernels, compute(): pl.pallas_call(compute_kernel, grid=(NLON,), out_shape=(jax.ShapeDtypeStr...  20.6 us
    unnamed x21, local copies, waits for them, and re-layouts  11.5 us

commit v1 on v0

v1 whole, which is shorter than its diff:
```python
import jax
import jax.numpy as jnp
from jax import lax
from jax.experimental import pallas as pl
from jax.experimental.pallas import tpu as pltpu
from jax.sharding import PartitionSpec as P

BS = 16
CAP = 2
C = 128
NLAT = 8
NLON = 16
RING = 4
BLK = 16
BLON = 8
HEIGHT = 32
WIDTH = 128
ROWS = BS + 2
TILES = ROWS + 4
EXT_ROWS = HEIGHT + 2
EXT_COLS = WIDTH + 2 * BS
MESH = pl.DeviceIdType.MESH
F32 = jnp.float32
BF16 = jnp.bfloat16


def peer_lon(me, k):
    z, y = me // RING, lax.rem(me, RING)
    return lax.rem(z + k // RING, RING) * RING + lax.rem(y + lax.rem(k, RING), RING)


def source_lon(me, k):
    z, y = me // RING, lax.rem(me, RING)
    return lax.rem(z + RING - k // RING, RING) * RING + lax.rem(y + RING - lax.rem(k, RING), RING)


def greet(lat, lon, diagonal):
    barrier = pltpu.get_barrier_semaphore()

    def signal(device):
        pl.semaphore_signal(barrier, inc=1, device_id=device, device_id_type=MESH)

    @pl.loop(1, NLON)
    def _(k):
        signal((lat, peer_lon(lon, k)))

    @pl.loop(1, NLAT)
    def _(k):
        signal((lax.rem(lat + k, NLAT), lon))

    for up, side in diagonal:
        signal((lax.rem(lat + up, NLAT), lax.rem(lon + side, NLON)))
    pl.semaphore_wait(barrier, NLON - 1 + NLAT - 1 + len(diagonal))


DIAGONAL = ((NLAT - 1, NLON - 1), (NLAT - 1, 1), (1, NLON - 1), (1, 1))


def index_tables(expert_ref, owner_ref, column, local, slot_block):
    for b in range(BLK):
        stored = owner_ref[expert_ref[b // BLON, b % BLON]]
        group = stored >> 1
        column[b] = group & (NLON - 1)
        local[b] = (group >> 4) * 2 + (stored & 1)

    @pl.loop(0, NLON)
    def _(c):
        first = jnp.int32(-1)
        second = jnp.int32(-1)
        for b in range(BLK):
            here = column[b] == c
            second = jnp.where(here & (first >= 0), b, second)
            first = jnp.where(here & (first < 0), b, first)
        slot_block[2 * c] = first
        slot_block[2 * c + 1] = second


def fused_kernel(
    expert_ref, owner_ref, fields, cot, bank,
    outputs, result, bank_out,
    column, local, slot_block, block_slot, ids, rank, order, final, canvas, ext, side_l, side_r,
    cot_in, patch_in, cot_stage, patch_stage, id_stage, got_cot, got_patch, got_id, kern,
    pad, taps, wide_cot, shift, total, running, out_stage, spread_stage, got_out, got_spread, block,
    pair_stage, got_pair, chip_stage, got_chip, row_in, col_in, corner_in,
    load_sem, cot_load, halo_send, halo_recv, bank_send, bank_recv, pass_send, pass_recv,
    cot_send, cot_recv, patch_send, patch_recv, id_send, id_recv,
    out_send, out_recv, spread_send, spread_recv, pair_sem, chip_send, chip_recv, edge_send, edge_recv,
    own_sem,
):
    lat, lon = lax.axis_index("lat"), lax.axis_index("lon")
    core = lax.rem(lat, 2)
    chip = lat // 2
    other = lat + 1 - 2 * core

    def remote(source, target, send, recv, device):
        return pltpu.make_async_remote_copy(
            source, target, send, recv, device_id=device, device_id_type=MESH
        )

    load_fields = pltpu.make_async_copy(
        fields, ext.at[pl.ds(1, HEIGHT), pl.ds(BS, WIDTH)], load_sem.at[0]
    )
    load_fields.start()
    load_bank = pltpu.make_async_copy(bank, kern.at[pl.ds(2 * lat, 2)], load_sem.at[1])
    load_bank.start()

    def load_cot(b):
        rows = pl.ds(pl.multiple_of((b // BLON) * BS, BS), BS)
        cols = pl.ds(pl.multiple_of(lax.rem(b, BLON) * BS, BS), BS)
        return pltpu.make_async_copy(cot.at[rows, cols], cot_in.at[b], cot_load.at[b])

    @pl.loop(0, BLK)
    def _(b):
        load_cot(b).start()

    index_tables(expert_ref, owner_ref, column, local, slot_block)
    for b in range(BLK):
        c = column[b]
        block_slot[b] = 2 * c + jnp.where(slot_block[2 * c + 1] == b, 1, 0)
    greet(lat, lon, DIAGONAL)

    up, down = lax.rem(lat + NLAT - 1, NLAT), lax.rem(lat + 1, NLAT)
    left, right = lax.rem(lon + NLON - 1, NLON), lax.rem(lon + 1, NLON)
    top, bottom = pl.ds(0, 1), pl.ds(HEIGHT - 1, 1)
    first, last = pl.ds(0, BS), pl.ds(WIDTH - BS, BS)
    all_rows, all_cols = pl.ds(0, HEIGHT), pl.ds(0, WIDTH)
    mid_rows, mid_cols = pl.ds(1, HEIGHT), pl.ds(BS, WIDTH)
    low, high = pl.ds(0, BS), pl.ds(BS + WIDTH, BS)
    zero, end = pl.ds(0, 1), pl.ds(EXT_ROWS - 1, 1)
    moves = (
        (top, all_cols, end, mid_cols, (up, lon)),
        (bottom, all_cols, zero, mid_cols, (down, lon)),
        (all_rows, first, mid_rows, high, (lat, left)),
        (all_rows, last, mid_rows, low, (lat, right)),
        (top, first, end, high, (up, left)),
        (top, last, end, low, (up, right)),
        (bottom, first, zero, high, (down, left)),
        (bottom, last, zero, low, (down, right)),
    )
    halos = []
    for i, (rows, cols, to_rows, to_cols, device) in enumerate(moves):
        copy = remote(
            fields.at[rows, cols], ext.at[to_rows, to_cols], halo_send.at[i], halo_recv.at[i], device
        )
        copy.start()
        halos.append(copy)

    def bank_copy(j):
        return remote(
            bank, kern.at[pl.ds(2 * lat, 2)], bank_send.at[j], bank_recv.at[j],
            (lax.rem(lat + 2 * j, NLAT), lon),
        )

    def pass_copy(j):
        part = kern.at[pl.ds(2 * lax.rem(lat + NLAT - 2 * j, NLAT), 2)]
        return remote(part, part, pass_send.at[j], pass_recv.at[j], (other, lon))

    share_bank = remote(
        bank, kern.at[pl.ds(2 * lat, 2)], pass_send.at[0], pass_recv.at[0], (other, lon)
    )
    for j in range(1, RING):
        bank_copy(j).start()
    share_bank.start()

    def cot_copy(k, r):
        dst = peer_lon(lon, k)
        return remote(
            cot_stage.at[dst, r], got_cot.at[2 * lon + r], cot_send.at[r, k], cot_recv.at[r, k], (lat, dst)
        )

    def patch_copy(k, r):
        dst = peer_lon(lon, k)
        return remote(
            patch_stage.at[dst, r], got_patch.at[2 * lon + r], patch_send.at[r, k], patch_recv.at[r, k],
            (lat, dst),
        )

    def id_copy(k):
        dst = peer_lon(lon, k)
        return remote(id_stage.at[dst], got_id.at[lon], id_send.at[k], id_recv.at[k], (lat, dst))

    def out_copy(k, r):
        dst = source_lon(lon, k)
        return remote(
            out_stage.at[2 * dst + r], got_out.at[2 * lon + r], out_send.at[r, k], out_recv.at[r, k], (lat, dst)
        )

    def spread_copy(k, r):
        dst = source_lon(lon, k)
        return remote(
            spread_stage.at[2 * dst + r], got_spread.at[2 * lon + r], spread_send.at[r, k],
            spread_recv.at[r, k], (lat, dst),
        )

    def own(source, target, i):
        return pltpu.make_async_copy(source, target, own_sem.at[i])

    own_slots = pl.ds(2 * lon, CAP)
    own_cot = own(cot_stage.at[lon], got_cot.at[own_slots], 0)
    own_patch = own(patch_stage.at[lon], got_patch.at[own_slots], 1)
    own_id = own(id_stage.at[lon], got_id.at[lon], 2)
    own_out = own(out_stage.at[own_slots], got_out.at[own_slots], 3)
    own_spread = own(spread_stage.at[own_slots], got_spread.at[own_slots], 4)

    lane = lax.broadcasted_iota(jnp.int32, (1, C), 1)

    @pl.loop(0, NLON)
    def _(c):
        found = [slot_block[2 * c + r] for r in range(CAP)]
        named = [jnp.where(f < 0, NLON, local[jnp.maximum(f, 0)]) for f in found]
        id_stage[c] = jnp.where(lane == 0, named[0], named[1])

    @pl.loop(1, NLON)
    def _(k):
        id_copy(k).start()

    @pl.loop(0, BLK)
    def _(b):
        load_cot(b).wait()

    def stage_cot(k, r):
        dst = peer_lon(lon, k)
        cot_stage[dst, r] = cot_in[jnp.maximum(slot_block[2 * dst + r], 0)]

    @pl.loop(1, NLON)
    def _(k):
        stage_cot(k, 0)
        cot_copy(k, 0).start()

    load_fields.wait()
    for copy in halos:
        copy.wait()

    @pl.when(lat == 0)
    def _():
        ext[0] = jnp.zeros((EXT_COLS, C), BF16)

    @pl.when(lat == NLAT - 1)
    def _():
        ext[EXT_ROWS - 1] = jnp.zeros((EXT_COLS, C), BF16)

    @pl.loop(0, EXT_ROWS)
    def _(r):
        canvas[pl.ds(pl.multiple_of(r * EXT_COLS, BS), EXT_COLS), :] = ext[r].astype(F32)

    @pl.loop(0, BLON)
    def _(k):
        side_l[k, pl.ds(0, EXT_ROWS)] = canvas[
            pl.ds(k * BS + BS - 1, EXT_ROWS, stride=EXT_COLS), :
        ].astype(BF16)
        side_r[k, pl.ds(0, EXT_ROWS)] = canvas[
            pl.ds(k * BS + 2 * BS, EXT_ROWS, stride=EXT_COLS), :
        ].astype(BF16)

    @pl.loop(0, BLK)
    def _(b):
        row = pl.multiple_of((b // BLON) * BS, BS)
        col = lax.rem(b, BLON)
        patch_in[b, pl.ds(0, ROWS)] = ext[
            pl.ds(row, ROWS), pl.ds(pl.multiple_of((col + 1) * BS, BS), BS), :
        ]
        patch_in[b, pl.ds(ROWS, 2)] = side_l[col, pl.ds(row, 2 * BS)].reshape(2, BS, C)
        patch_in[b, pl.ds(ROWS + 2, 2)] = side_r[col, pl.ds(row, 2 * BS)].reshape(2, BS, C)

    def stage_patch(k, r):
        dst = peer_lon(lon, k)
        patch_stage[dst, r] = patch_in[jnp.maximum(slot_block[2 * dst + r], 0)]

    @pl.loop(1, NLON)
    def _(k):
        stage_patch(k, 0)
        patch_copy(k, 0).start()

    @pl.loop(1, NLON)
    def _(k):
        stage_cot(k, 1)
        cot_copy(k, 1).start()

    @pl.loop(1, NLON)
    def _(k):
        stage_patch(k, 1)
        patch_copy(k, 1).start()

    for r in range(CAP):
        stage_cot(0, r)
        stage_patch(0, r)
    own_cot.start()
    own_patch.start()
    own_id.start()

    load_bank.wait()
    for j in range(1, RING):
        bank_copy(j).wait()
        pass_copy(j).start()

    own_id.wait()

    @pl.loop(1, NLON)
    def _(k):
        id_copy(k).wait()

    read_ids = pltpu.make_async_copy(got_id, ids, load_sem.at[2])
    read_ids.start()
    read_ids.wait()
    canvas[...] = jnp.zeros_like(canvas)
    wide_cot[...] = jnp.zeros_like(wide_cot)

    @pl.loop(0, NLON)
    def _(c):
        for r in range(CAP):
            mine = ids[c, 0, r]
            here = 2 * c + r
            before = jnp.int32(0)
            for s in range(NLON * CAP):
                it = ids[s // CAP, 0, s % CAP]
                before += jnp.where((it < mine) | ((it == mine) & (s < here)), 1, 0)
            rank[here] = before

    @pl.loop(0, NLON * CAP)
    def _(j):
        slot = jnp.int32(0)
        for s in range(NLON * CAP):
            slot = jnp.where(rank[s] == j, s, slot)
        order[j] = slot

    @pl.loop(0, NLON)
    def _(e):
        upto = jnp.int32(0)
        some = jnp.int32(0)
        for s in range(NLON * CAP):
            it = ids[s // CAP, 0, s % CAP]
            upto += jnp.where(it <= e, 1, 0)
            some += jnp.where(it == e, 1, 0)
        final[e] = jnp.where(some > 0, upto - 1, -1)

    share_bank.wait()
    for j in range(1, RING):
        pass_copy(j).wait()

    def build_taps(slot):
        pad[:, pl.ds(8, BS), :] = got_patch[slot, pl.ds(0, ROWS)].astype(F32)
        pad[:, 7, :] = got_patch[slot, pl.ds(ROWS, 2)].reshape(2 * BS, C)[:ROWS].astype(F32)
        pad[:, BS + 8, :] = got_patch[slot, pl.ds(ROWS + 2, 2)].reshape(2 * BS, C)[:ROWS].astype(F32)
        for b in range(3):
            taps[:, pl.ds(b * C, C)] = pad[:, pl.ds(7 + b, BS), :].reshape(ROWS * BS, C).astype(BF16)

    def convolve(slot, e):
        build_taps(slot)
        cots = got_cot[slot].reshape(BS * BS, C)
        for a in range(3):
            wide_cot[pl.ds(a * BS, BS * BS), pl.ds(a * C, C)] = cots
        weights = [kern[e, pl.ds(3 * a, 3)].reshape(3 * C, C) for a in range(3)]
        sums = jnp.zeros((BS * BS, C), F32)
        for a in range(3):
            sums += jnp.dot(taps[pl.ds(a * BS, BS * BS), :], weights[a], preferred_element_type=F32)
        out_stage[slot] = sums.astype(BF16).reshape(BS, BS, C)
        grid = lax.dot_general(
            wide_cot[...], jnp.concatenate(weights, axis=1), (((1,), (1,)), ((), ())),
            preferred_element_type=F32,
        )
        shift[0, :, pl.ds(8, BS), :] = grid[:, :C].reshape(ROWS, BS, C)
        shift[1, :, pl.ds(8, BS), :] = grid[:, 2 * C:].reshape(ROWS, BS, C)
        place = lax.broadcasted_iota(jnp.int32, (ROWS, BS, C), 1)
        main = grid[:, C:2 * C].reshape(ROWS, BS, C)
        main += jnp.where(place == BS - 1, 0.0, shift[0, :, pl.ds(9, BS), :])
        main += jnp.where(place == 0, 0.0, shift[1, :, pl.ds(7, BS), :])
        spread_stage[slot, pl.ds(0, ROWS)] = main.astype(BF16)
        tail = jnp.zeros((2 * BS - ROWS, C), F32)
        lefts = jnp.concatenate([shift[0, :, 8, :], tail], axis=0)
        rights = jnp.concatenate([shift[1, :, BS + 7, :], tail], axis=0)
        spread_stage[slot, pl.ds(ROWS, 2)] = lefts.astype(BF16).reshape(2, BS, C)
        spread_stage[slot, pl.ds(ROWS + 2, 2)] = rights.astype(BF16).reshape(2, BS, C)

    own_cot.wait()
    own_patch.wait()

    @pl.loop(0, CAP * NLON)
    def _(step):
        r, k = step // NLON, lax.rem(step, NLON)
        source = source_lon(lon, k)

        @pl.when(k > 0)
        def _():
            cot_copy(k, r).wait_recv()
            patch_copy(k, r).wait_recv()

        convolve(2 * source + r, jnp.minimum(ids[source, 0, r], NLON - 1))

        @pl.when(k > 0)
        def _():
            spread_copy(k, r).start()

        @pl.when((k > 0) & (r == 0))
        def _():
            out_copy(k, r).start()

    @pl.loop(1, NLON)
    def _(k):
        out_copy(k, 1).start()

    own_out.start()
    own_spread.start()

    @pl.loop(0, NLON * CAP)
    def _(j):
        slot = order[j]
        previous = order[jnp.maximum(j - 1, 0)]
        now = ids[slot >> 1, 0, slot & 1]
        same = (j > 0) & (ids[previous >> 1, 0, previous & 1] == now)
        build_taps(slot)
        cots = got_cot[slot].reshape(BS * BS, C)
        for a in range(3):
            term = lax.dot_general(
                taps[pl.ds(a * BS, BS * BS), :], cots, (((0,), (0,)), ((), ())),
                preferred_element_type=F32,
            ).reshape(3, C, C)
            sums = jnp.where(same, total[pl.ds(3 * a, 3)], 0.0) + term
            total[pl.ds(3 * a, 3)] = sums
            running[j, pl.ds(3 * a, 3)] = sums.astype(BF16)

    def gradient(e):
        at = final[e]
        return jnp.where(at < 0, 0.0, running[jnp.maximum(at, 0)].astype(F32))

    @pl.loop(0, NLAT)
    def _(i):
        e = 4 * (i // 2) + 2 * (1 - core) + lax.rem(i, 2)
        pair_stage[i] = gradient(e).astype(BF16)

    pair = remote(pair_stage, got_pair, pair_sem.at[0], pair_sem.at[1], (other, lon))
    pair.start()

    def chip_copy(j):
        to = lax.rem(chip + j, RING)
        return remote(
            chip_stage.at[to], got_chip.at[chip], chip_send.at[j], chip_recv.at[j], (2 * to + core, lon)
        )

    pair.wait()

    @pl.loop(1, RING)
    def _(j):
        to = lax.rem(chip + j, RING)
        for i in range(2):
            both = gradient(4 * to + 2 * core + i) + got_pair[2 * to + i].astype(F32)
            chip_stage[to, i] = both.astype(BF16)
        chip_copy(j).start()

    for i in range(2):
        bank_out[i] = gradient(4 * chip + 2 * core + i) + got_pair[2 * chip + i].astype(F32)

    own_spread.wait()

    @pl.loop(1, NLON)
    def _(k):
        for r in range(CAP):
            spread_copy(k, r).wait_recv()

    @pl.loop(0, BLK)
    def _(b):
        bi, bj = b // BLON, lax.rem(b, BLON)
        base = bi * BS * EXT_COLS + (bj + 1) * BS
        block[...] = got_spread[block_slot[b]]

        @pl.loop(0, ROWS)
        def _(i):
            at = pl.ds(pl.multiple_of(base + i * EXT_COLS, BS), BS)
            canvas[at, :] += block[i].astype(F32)

        lefts = block[pl.ds(ROWS, 2)].reshape(2 * BS, C)[:ROWS].astype(F32)
        rights = block[pl.ds(ROWS + 2, 2)].reshape(2 * BS, C)[:ROWS].astype(F32)
        canvas[pl.ds(base - 1, ROWS, stride=EXT_COLS), :] += lefts
        canvas[pl.ds(base + BS, ROWS, stride=EXT_COLS), :] += rights

    grid = canvas.reshape(EXT_ROWS, EXT_COLS, C)
    half = BS // 2
    edge_low, edge_high = pl.ds(half, half), pl.ds(BS + WIDTH, half)
    edges = (
        (grid.at[0, mid_cols], row_in.at[0], (up, lon)),
        (grid.at[EXT_ROWS - 1, mid_cols], row_in.at[1], (down, lon)),
        (grid.at[mid_rows, edge_low], col_in.at[0], (lat, left)),
        (grid.at[mid_rows, edge_high], col_in.at[1], (lat, right)),
        (grid.at[0, edge_low], corner_in.at[0], (up, left)),
        (grid.at[0, edge_high], corner_in.at[1], (up, right)),
        (grid.at[EXT_ROWS - 1, edge_low], corner_in.at[2], (down, left)),
        (grid.at[EXT_ROWS - 1, edge_high], corner_in.at[3], (down, right)),
    )
    edge_copies = []
    for i, (source, target, device) in enumerate(edges):
        copy = remote(source, target, edge_send.at[i], edge_recv.at[i], device)
        copy.start()
        edge_copies.append(copy)

    @pl.loop(1, RING)
    def _(j):
        chip_copy(j).wait()
        back = lax.rem(chip + RING - j, RING)
        for i in range(2):
            bank_out[i] += got_chip[back, i].astype(F32)

    own_out.wait()

    @pl.loop(1, NLON)
    def _(k):
        for r in range(CAP):
            out_copy(k, r).wait_recv()

    @pl.loop(0, BLK)
    def _(b):
        bi, bj = b // BLON, lax.rem(b, BLON)
        outputs[
            pl.ds(pl.multiple_of(bi * BS, BS), BS), pl.ds(pl.multiple_of(bj * BS, BS), BS), :
        ] = got_out[block_slot[b]]

    for copy in edge_copies:
        copy.wait()
    from_down = jnp.where(lat < NLAT - 1, 1.0, 0.0).astype(F32)
    from_up = jnp.where(lat > 0, 1.0, 0.0).astype(F32)
    upper, lower = EXT_COLS, HEIGHT * EXT_COLS
    canvas[pl.ds(lower + BS, WIDTH), :] += row_in[0] * from_down
    canvas[pl.ds(upper + BS, WIDTH), :] += row_in[1] * from_up

    @pl.loop(0, HEIGHT)
    def _(i):
        start = pl.multiple_of((i + 1) * EXT_COLS, BS)
        canvas[pl.ds(start + BS + WIDTH - half, half), :] += col_in[0, i]
        canvas[pl.ds(start + BS, half), :] += col_in[1, i]

    canvas[pl.ds(lower + BS + WIDTH - half, half), :] += corner_in[0] * from_down
    canvas[pl.ds(lower + BS, half), :] += corner_in[1] * from_down
    canvas[pl.ds(upper + BS + WIDTH - half, half), :] += corner_in[2] * from_up
    canvas[pl.ds(upper + BS, half), :] += corner_in[3] * from_up

    @pl.loop(0, HEIGHT)
    def _(i):
        start = pl.multiple_of((i + 1) * EXT_COLS + BS, BS)
        result[i] = canvas[pl.ds(start, WIDTH), :].astype(BF16)

    @pl.loop(1, NLON)
    def _(k):
        for r in range(CAP):
            cot_copy(k, r).wait_send()
            patch_copy(k, r).wait_send()
            spread_copy(k, r).wait_send()
            out_copy(k, r).wait_send()


def local(fields, cotangent, kernel_bank, block_expert, owner):
    hbm = pl.BlockSpec(memory_space=pltpu.HBM)
    smem = pl.BlockSpec(memory_space=pltpu.SMEM)
    vmem = pl.BlockSpec(memory_space=pltpu.VMEM)
    dma = pltpu.SemaphoreType.DMA
    slots = NLON * CAP
    return pl.pallas_call(
        fused_kernel,
        out_shape=(
            jax.ShapeDtypeStruct((HEIGHT, WIDTH, C), BF16),
            jax.ShapeDtypeStruct((HEIGHT, WIDTH, C), BF16),
            jax.ShapeDtypeStruct((2, 9, C, C), F32),
        ),
        in_specs=[smem, smem, hbm, hbm, hbm],
        out_specs=(vmem, vmem, vmem),
        scratch_shapes=[
            pltpu.SMEM((BLK,), jnp.int32),
            pltpu.SMEM((BLK,), jnp.int32),
            pltpu.SMEM((slots,), jnp.int32),
            pltpu.SMEM((BLK,), jnp.int32),
            pltpu.SMEM((NLON, 1, C), jnp.int32),
            pltpu.SMEM((slots,), jnp.int32),
            pltpu.SMEM((slots,), jnp.int32),
            pltpu.SMEM((NLON,), jnp.int32),
            pltpu.VMEM((EXT_ROWS * EXT_COLS, C), F32),
            pltpu.VMEM((EXT_ROWS, EXT_COLS, C), BF16),
            pltpu.VMEM((BLON, 3 * BS, C), BF16),
            pltpu.VMEM((BLON, 3 * BS, C), BF16),
            pltpu.VMEM((BLK, BS, BS, C), BF16),
            pltpu.VMEM((BLK, TILES, BS, C), BF16),
            pltpu.VMEM((NLON, CAP, BS, BS, C), BF16),
            pltpu.VMEM((NLON, CAP, TILES, BS, C), BF16),
            pltpu.VMEM((NLON, 1, C), jnp.int32),
            pltpu.VMEM((slots, BS, BS, C), BF16),
            pltpu.VMEM((slots, TILES, BS, C), BF16),
            pltpu.VMEM((NLON, 1, C), jnp.int32),
            pltpu.VMEM((NLON, 9, C, C), BF16),
            pltpu.VMEM((ROWS, 2 * BS, C), F32),
            pltpu.VMEM((ROWS * BS, 3 * C), BF16),
            pltpu.VMEM((ROWS * BS, 3 * C), BF16),
            pltpu.VMEM((2, ROWS, 2 * BS, C), F32),
            pltpu.VMEM((9, C, C), F32),
            pltpu.VMEM((slots, 9, C, C), BF16),
            pltpu.VMEM((slots, BS, BS, C), BF16),
            pltpu.VMEM((slots, TILES, BS, C), BF16),
            pltpu.VMEM((slots, BS, BS, C), BF16),
            pltpu.VMEM((slots, TILES, BS, C), BF16),
            pltpu.VMEM((TILES, BS, C), BF16),
            pltpu.VMEM((NLAT, 9, C, C), BF16),
            pltpu.VMEM((NLAT, 9, C, C), BF16),
            pltpu.VMEM((RING, 2, 9, C, C), BF16),
            pltpu.VMEM((RING, 2, 9, C, C), BF16),
            pltpu.VMEM((2, WIDTH, C), F32),
            pltpu.VMEM((2, HEIGHT, BS // 2, C), F32),
            pltpu.VMEM((4, BS // 2, C), F32),
            dma((3,)), dma((BLK,)),
            dma((8,)), dma((8,)),
            dma((RING,)), dma((RING,)),
            dma((RING,)), dma((RING,)),
            dma((CAP, NLON)), dma((CAP, NLON)),
            dma((CAP, NLON)), dma((CAP, NLON)),
            dma((NLON,)), dma((NLON,)),
            dma((CAP, NLON)), dma((CAP, NLON)),
            dma((CAP, NLON)), dma((CAP, NLON)),
            dma((2,)),
            dma((RING,)), dma((RING,)),
            dma((8,)), dma((8,)),
            dma((5,)),
        ],
        compiler_params=pltpu.CompilerParams(
            collective_id=0, has_side_effects=True, vmem_limit_bytes=62 << 20
        ),
    )(block_expert, owner, fields, cotangent, kernel_bank)


def solution(mesh):
    return jax.shard_map(
        local,
        mesh=mesh,
        in_specs=(
            P("lat", "lon", None),
            P("lat", "lon", None),
            P(("lat", "lon"), None, None, None),
            P("lat", "lon"),
            P(),
        ),
        out_specs=(
            P("lat", "lon", None),
            P("lat", "lon", None),
            P(("lat", "lon"), None, None, None),
        ),
        check_vma=False,
    )
```

time: 188 us -> 153 us (0.81)
  Pallas kernels: 175 us -> 146 us
  local copies, waits for them, and re-layouts: 11.5 us -> 5.06 us
    pallas_call x3 -> x1, Pallas kernels: 175 us -> 146 us  [local(): pl.pallas_call(fused_kernel, out_shape=(jax.ShapeDtypeStruct((HEIGHT, WID...]
    unnamed x21 -> x7, local copies, waits for them, and re-layouts: 11.5 us -> 5.06 us
where the time goes in v1:
time: 153 us; the launch traced here: 152 us
  Pallas kernels  146 us (95%)
  local copies, waits for them, and re-layouts  5.06 us (3%)
    pallas_call x1, Pallas kernels, local(): pl.pallas_call(fused_kernel, out_shape=(jax.ShapeDtypeStruct((HEIGHT, WID...  146 us
    unnamed x7, local copies, waits for them, and re-layouts  5.06 us

profile of v1, /device:TPU:1, one launch (start us, length us, event | category | flops | bytes accessed | tf_op | source)
XLA Modules:
  0.0 151.7 jit_solution(11412299552514559426)
XLA Ops:
  0.6 145.9 %shard_map.76 = (bf16[32,128,128]{2,1,0:T(8,128)(2,1)}, bf16[32,128,128]{2,1,0:T(8,128)(2,1)}, f32[2,9,128,128]{3,2,1,0:T(8,128)}) custom-call(s32[2,8]{1,0:T(2,128)} %expert_ref.1, s32[256]{0:T(256)} %owner_ref.1, bf16[32,128,128]{2,1,0:T(8,128)(2,1)} %fields.1, bf16[32,128,128]{2,1,0:T(8,128)(2,1)} %cot.1, bf16[2,9,128,128]{3,2,1,0:T(8,128)(2,1)} %bank.1), custom_call_target="tpu_custom_call" | custom-call | tf_op jit(solution)/shard_map/pallas_call | solution.py:554
  146.6 0.0 copy-start.1
  146.6 2.4 %copy.11 = bf16[32,128,128]{2,1,0:T(8,128)(2,1)} copy(bf16[32,128,128]{2,1,0:T(8,128)(2,1)} %get-tuple-element.6) | data formatting | bytes 2097152
  149.0 0.0 copy-done.1
  149.0 0.0 copy-start
  149.0 1.0 copy.12
  150.0 0.7 copy-done
  150.6 1.0 copy.13
Async XLA Ops:
  146.6 2.4 %copy-start.1 = (bf16[32,128,128]{2,1,0:T(8,128)(2,1)S(1)}, bf16[32,128,128]{2,1,0:T(8,128)(2,1)}, u32[]{:S(2)}) copy-start(bf16[32,128,128]{2,1,0:T(8,128)(2,1)} %get-tuple-element.7) | copy-start | bytes 3145732
  149.0 1.6 %copy-start = (f32[2,9,128,128]{3,2,1,0:T(8,128)S(1)}, f32[2,9,128,128]{3,2,1,0:T(8,128)}, u32[]{:S(2)}) copy-start(f32[2,9,128,128]{3,2,1,0:T(8,128)} %get-tuple-element.8) | copy-start | bytes 3538948

commit v2 on v1

--- a/solution.py
+++ b/solution.py
@@ -16,7 +16,8 @@
 HEIGHT = 32
 WIDTH = 128
 ROWS = BS + 2
-TILES = ROWS + 4
+SIDE = 24
+TILES = ROWS + 3
 EXT_ROWS = HEIGHT + 2
 EXT_COLS = WIDTH + 2 * BS
 MESH = pl.DeviceIdType.MESH
@@ -50,7 +51,10 @@
 
     for up, side in diagonal:
         signal((lax.rem(lat + up, NLAT), lax.rem(lon + side, NLON)))
-    pl.semaphore_wait(barrier, NLON - 1 + NLAT - 1 + len(diagonal))
+
+
+def await_greetings(diagonal):
+    pl.semaphore_wait(pltpu.get_barrier_semaphore(), NLON - 1 + NLAT - 1 + len(diagonal))
 
 
 DIAGONAL = ((NLAT - 1, NLON - 1), (NLAT - 1, 1), (1, NLON - 1), (1, 1))
@@ -78,8 +82,8 @@
 def fused_kernel(
     expert_ref, owner_ref, fields, cot, bank,
     outputs, result, bank_out,
-    column, local, slot_block, block_slot, ids, rank, order, final, canvas, ext, side_l, side_r,
-    cot_in, patch_in, cot_stage, patch_stage, id_stage, got_cot, got_patch, got_id, kern,
+    home, local, slot_block, block_slot, ids, rank, order, final, canvas, ext,
+    col_stage, col_got, side_stage, sides, cot_in, patch_in, cot_stage, patch_stage, id_stage, got_cot, got_patch, got_id, kern,
     pad, taps, wide_cot, shift, total, running, out_stage, spread_stage, got_out, got_spread, block,
     pair_stage, got_pair, chip_stage, got_chip, row_in, col_in, corner_in,
     load_sem, cot_load, halo_send, halo_recv, bank_send, bank_recv, pass_send, pass_recv,
@@ -97,6 +101,7 @@
             source, target, send, recv, device_id=device, device_id_type=MESH
         )
 
+    greet(lat, lon, DIAGONAL)
     load_fields = pltpu.make_async_copy(
         fields, ext.at[pl.ds(1, HEIGHT), pl.ds(BS, WIDTH)], load_sem.at[0]
     )
@@ -113,25 +118,22 @@
     def _(b):
         load_cot(b).start()
 
-    index_tables(expert_ref, owner_ref, column, local, slot_block)
+    index_tables(expert_ref, owner_ref, home, local, slot_block)
     for b in range(BLK):
-        c = column[b]
+        c = home[b]
         block_slot[b] = 2 * c + jnp.where(slot_block[2 * c + 1] == b, 1, 0)
-    greet(lat, lon, DIAGONAL)
+    await_greetings(DIAGONAL)
 
     up, down = lax.rem(lat + NLAT - 1, NLAT), lax.rem(lat + 1, NLAT)
     left, right = lax.rem(lon + NLON - 1, NLON), lax.rem(lon + 1, NLON)
     top, bottom = pl.ds(0, 1), pl.ds(HEIGHT - 1, 1)
     first, last = pl.ds(0, BS), pl.ds(WIDTH - BS, BS)
-    all_rows, all_cols = pl.ds(0, HEIGHT), pl.ds(0, WIDTH)
-    mid_rows, mid_cols = pl.ds(1, HEIGHT), pl.ds(BS, WIDTH)
+    all_cols, mid_cols = pl.ds(0, WIDTH), pl.ds(BS, WIDTH)
     low, high = pl.ds(0, BS), pl.ds(BS + WIDTH, BS)
     zero, end = pl.ds(0, 1), pl.ds(EXT_ROWS - 1, 1)
     moves = (
         (top, all_cols, end, mid_cols, (up, lon)),
         (bottom, all_cols, zero, mid_cols, (down, lon)),
-        (all_rows, first, mid_rows, high, (lat, left)),
-        (all_rows, last, mid_rows, low, (lat, right)),
         (top, first, end, high, (up, left)),
         (top, last, end, low, (up, right)),
         (bottom, first, zero, high, (down, left)),
@@ -145,6 +147,26 @@
         copy.start()
         halos.append(copy)
 
+    def column(where):
+        return pl.ds(EXT_COLS + where, HEIGHT, stride=EXT_COLS)
+
+    outer_left, inner_left, inner_right, outer_right = BS - 1, BS, BS + WIDTH - 1, BS + WIDTH
+    load_fields.wait()
+
+    def widen(r):
+        canvas[pl.ds(pl.multiple_of(r * EXT_COLS, BS), EXT_COLS), :] = ext[r].astype(F32)
+
+    @pl.loop(1, HEIGHT + 1)
+    def _(r):
+        widen(r)
+
+    col_stage[0] = canvas[column(inner_left), :].astype(BF16)
+    col_stage[1] = canvas[column(inner_right), :].astype(BF16)
+    for i, device in enumerate(((lat, left), (lat, right))):
+        copy = remote(col_stage.at[i], col_got.at[i], halo_send.at[6 + i], halo_recv.at[6 + i], device)
+        copy.start()
+        halos.append(copy)
+
     def bank_copy(j):
         return remote(
             bank, kern.at[pl.ds(2 * lat, 2)], bank_send.at[j], bank_recv.at[j],
@@ -227,7 +249,6 @@
         stage_cot(k, 0)
         cot_copy(k, 0).start()
 
-    load_fields.wait()
     for copy in halos:
         copy.wait()
 
@@ -239,28 +260,20 @@
     def _():
         ext[EXT_ROWS - 1] = jnp.zeros((EXT_COLS, C), BF16)
 
-    @pl.loop(0, EXT_ROWS)
-    def _(r):
-        canvas[pl.ds(pl.multiple_of(r * EXT_COLS, BS), EXT_COLS), :] = ext[r].astype(F32)
-
-    @pl.loop(0, BLON)
-    def _(k):
-        side_l[k, pl.ds(0, EXT_ROWS)] = canvas[
-            pl.ds(k * BS + BS - 1, EXT_ROWS, stride=EXT_COLS), :
-        ].astype(BF16)
-        side_r[k, pl.ds(0, EXT_ROWS)] = canvas[
-            pl.ds(k * BS + 2 * BS, EXT_ROWS, stride=EXT_COLS), :
-        ].astype(BF16)
+    widen(0)
+    widen(EXT_ROWS - 1)
+    canvas[column(outer_right), :] = col_got[0].astype(F32)
+    canvas[column(outer_left), :] = col_got[1].astype(F32)
 
     @pl.loop(0, BLK)
     def _(b):
         row = pl.multiple_of((b // BLON) * BS, BS)
-        col = lax.rem(b, BLON)
-        patch_in[b, pl.ds(0, ROWS)] = ext[
-            pl.ds(row, ROWS), pl.ds(pl.multiple_of((col + 1) * BS, BS), BS), :
-        ]
-        patch_in[b, pl.ds(ROWS, 2)] = side_l[col, pl.ds(row, 2 * BS)].reshape(2, BS, C)
-        patch_in[b, pl.ds(ROWS + 2, 2)] = side_r[col, pl.ds(row, 2 * BS)].reshape(2, BS, C)
+        col = pl.multiple_of((lax.rem(b, BLON) + 1) * BS, BS)
+        patch_in[b, pl.ds(0, ROWS)] = ext[pl.ds(row, ROWS), pl.ds(col, BS), :]
+        start = row * EXT_COLS + col
+        sides[pl.ds(0, ROWS), :] = canvas[pl.ds(start - 1, ROWS, stride=EXT_COLS), :]
+        sides[pl.ds(SIDE, ROWS), :] = canvas[pl.ds(start + BS, ROWS, stride=EXT_COLS), :]
+        patch_in[b, pl.ds(ROWS, 3)] = sides[...].astype(BF16).reshape(3, BS, C)
 
     def stage_patch(k, r):
         dst = peer_lon(lon, k)
@@ -339,8 +352,9 @@
 
     def build_taps(slot):
         pad[:, pl.ds(8, BS), :] = got_patch[slot, pl.ds(0, ROWS)].astype(F32)
-        pad[:, 7, :] = got_patch[slot, pl.ds(ROWS, 2)].reshape(2 * BS, C)[:ROWS].astype(F32)
-        pad[:, BS + 8, :] = got_patch[slot, pl.ds(ROWS + 2, 2)].reshape(2 * BS, C)[:ROWS].astype(F32)
+        both = got_patch[slot, pl.ds(ROWS, 3)].reshape(3 * BS, C).astype(F32)
+        pad[:, 7, :] = both[:ROWS]
+        pad[:, BS + 8, :] = both[SIDE:SIDE + ROWS]
         for b in range(3):
             taps[:, pl.ds(b * C, C)] = pad[:, pl.ds(7 + b, BS), :].reshape(ROWS * BS, C).astype(BF16)
 
@@ -365,11 +379,9 @@
         main += jnp.where(place == BS - 1, 0.0, shift[0, :, pl.ds(9, BS), :])
         main += jnp.where(place == 0, 0.0, shift[1, :, pl.ds(7, BS), :])
         spread_stage[slot, pl.ds(0, ROWS)] = main.astype(BF16)
-        tail = jnp.zeros((2 * BS - ROWS, C), F32)
-        lefts = jnp.concatenate([shift[0, :, 8, :], tail], axis=0)
-        rights = jnp.concatenate([shift[1, :, BS + 7, :], tail], axis=0)
-        spread_stage[slot, pl.ds(ROWS, 2)] = lefts.astype(BF16).reshape(2, BS, C)
-        spread_stage[slot, pl.ds(ROWS + 2, 2)] = rights.astype(BF16).reshape(2, BS, C)
+        sides[pl.ds(0, ROWS), :] = shift[0, :, 8, :]
+        sides[pl.ds(SIDE, ROWS), :] = shift[1, :, BS + 7, :]
+        spread_stage[slot, pl.ds(ROWS, 3)] = sides[...].astype(BF16).reshape(3, BS, C)
 
     own_cot.wait()
     own_patch.wait()
@@ -462,24 +474,23 @@
         base = bi * BS * EXT_COLS + (bj + 1) * BS
         block[...] = got_spread[block_slot[b]]
 
-        @pl.loop(0, ROWS)
-        def _(i):
+        for i in range(ROWS):
             at = pl.ds(pl.multiple_of(base + i * EXT_COLS, BS), BS)
             canvas[at, :] += block[i].astype(F32)
-
-        lefts = block[pl.ds(ROWS, 2)].reshape(2 * BS, C)[:ROWS].astype(F32)
-        rights = block[pl.ds(ROWS + 2, 2)].reshape(2 * BS, C)[:ROWS].astype(F32)
-        canvas[pl.ds(base - 1, ROWS, stride=EXT_COLS), :] += lefts
-        canvas[pl.ds(base + BS, ROWS, stride=EXT_COLS), :] += rights
-
+        both = block[pl.ds(ROWS, 3)].reshape(3 * BS, C).astype(F32)
+        canvas[pl.ds(base - 1, ROWS, stride=EXT_COLS), :] += both[:ROWS]
+        canvas[pl.ds(base + BS, ROWS, stride=EXT_COLS), :] += both[SIDE:SIDE + ROWS]
+
+    side_stage[0] = canvas[column(outer_left), :]
+    side_stage[1] = canvas[column(outer_right), :]
     grid = canvas.reshape(EXT_ROWS, EXT_COLS, C)
     half = BS // 2
     edge_low, edge_high = pl.ds(half, half), pl.ds(BS + WIDTH, half)
     edges = (
         (grid.at[0, mid_cols], row_in.at[0], (up, lon)),
         (grid.at[EXT_ROWS - 1, mid_cols], row_in.at[1], (down, lon)),
-        (grid.at[mid_rows, edge_low], col_in.at[0], (lat, left)),
-        (grid.at[mid_rows, edge_high], col_in.at[1], (lat, right)),
+        (side_stage.at[0], col_in.at[0], (lat, left)),
+        (side_stage.at[1], col_in.at[1], (lat, right)),
         (grid.at[0, edge_low], corner_in.at[0], (up, left)),
         (grid.at[0, edge_high], corner_in.at[1], (up, right)),
         (grid.at[EXT_ROWS - 1, edge_low], corner_in.at[2], (down, left)),
@@ -512,6 +523,14 @@
             pl.ds(pl.multiple_of(bi * BS, BS), BS), pl.ds(pl.multiple_of(bj * BS, BS), BS), :
         ] = got_out[block_slot[b]]
 
+    def round_cells(i, col, count):
+        start = pl.multiple_of((i + 1) * EXT_COLS + BS + col, BS)
+        result[i, pl.ds(col, count)] = canvas[pl.ds(start, count), :].astype(BF16)
+
+    @pl.loop(1, HEIGHT - 1)
+    def _(i):
+        round_cells(i, BS, WIDTH - 2 * BS)
+
     for copy in edge_copies:
         copy.wait()
     from_down = jnp.where(lat < NLAT - 1, 1.0, 0.0).astype(F32)
@@ -520,21 +539,20 @@
     canvas[pl.ds(lower + BS, WIDTH), :] += row_in[0] * from_down
     canvas[pl.ds(upper + BS, WIDTH), :] += row_in[1] * from_up
 
-    @pl.loop(0, HEIGHT)
-    def _(i):
-        start = pl.multiple_of((i + 1) * EXT_COLS, BS)
-        canvas[pl.ds(start + BS + WIDTH - half, half), :] += col_in[0, i]
-        canvas[pl.ds(start + BS, half), :] += col_in[1, i]
-
+    canvas[column(inner_right), :] += col_in[0]
+    canvas[column(inner_left), :] += col_in[1]
     canvas[pl.ds(lower + BS + WIDTH - half, half), :] += corner_in[0] * from_down
     canvas[pl.ds(lower + BS, half), :] += corner_in[1] * from_down
     canvas[pl.ds(upper + BS + WIDTH - half, half), :] += corner_in[2] * from_up
     canvas[pl.ds(upper + BS, half), :] += corner_in[3] * from_up
 
-    @pl.loop(0, HEIGHT)
+    for i in (0, HEIGHT - 1):
+        round_cells(i, 0, WIDTH)
+
+    @pl.loop(1, HEIGHT - 1)
     def _(i):
-        start = pl.multiple_of((i + 1) * EXT_COLS + BS, BS)
-        result[i] = canvas[pl.ds(start, WIDTH), :].astype(BF16)
+        round_cells(i, 0, BS)
+        round_cells(i, WIDTH - BS, BS)
 
     @pl.loop(1, NLON)
     def _(k):
@@ -543,6 +561,15 @@
             patch_copy(k, r).wait_send()
             spread_copy(k, r).wait_send()
             out_copy(k, r).wait_send()
+
+
+def write_kernel(a, b, c, a_out, b_out, c_out, sem):
+    pairs = ((a, a_out), (b, b_out), (c, c_out))
+    copies = [pltpu.make_async_copy(x, y, sem.at[i]) for i, (x, y) in enumerate(pairs)]
+    for copy in copies:
+        copy.start()
+    for copy in copies:
+        copy.wait()
 
 
 def local(fields, cotangent, kernel_bank, block_expert, owner):
@@ -551,7 +578,7 @@
     vmem = pl.BlockSpec(memory_space=pltpu.VMEM)
     dma = pltpu.SemaphoreType.DMA
     slots = NLON * CAP
-    return pl.pallas_call(
+    results = pl.pallas_call(
         fused_kernel,
         out_shape=(
             jax.ShapeDtypeStruct((HEIGHT, WIDTH, C), BF16),
@@ -571,8 +598,10 @@
             pltpu.SMEM((NLON,), jnp.int32),
             pltpu.VMEM((EXT_ROWS * EXT_COLS, C), F32),
             pltpu.VMEM((EXT_ROWS, EXT_COLS, C), BF16),
-            pltpu.VMEM((BLON, 3 * BS, C), BF16),
-            pltpu.VMEM((BLON, 3 * BS, C), BF16),
+            pltpu.VMEM((2, HEIGHT, C), BF16),
+            pltpu.VMEM((2, HEIGHT, C), BF16),
+            pltpu.VMEM((2, HEIGHT, C), F32),
+            pltpu.VMEM((3 * BS, C), F32),
             pltpu.VMEM((BLK, BS, BS, C), BF16),
             pltpu.VMEM((BLK, TILES, BS, C), BF16),
             pltpu.VMEM((NLON, CAP, BS, BS, C), BF16),
@@ -598,7 +627,7 @@
             pltpu.VMEM((RING, 2, 9, C, C), BF16),
             pltpu.VMEM((RING, 2, 9, C, C), BF16),
             pltpu.VMEM((2, WIDTH, C), F32),
-            pltpu.VMEM((2, HEIGHT, BS // 2, C), F32),
+            pltpu.VMEM((2, HEIGHT, C), F32),
             pltpu.VMEM((4, BS // 2, C), F32),
             dma((3,)), dma((BLK,)),
             dma((8,)), dma((8,)),
@@ -618,6 +647,13 @@
             collective_id=0, has_side_effects=True, vmem_limit_bytes=62 << 20
         ),
     )(block_expert, owner, fields, cotangent, kernel_bank)
+    return pl.pallas_call(
+        write_kernel,
+        out_shape=tuple(jax.ShapeDtypeStruct(x.shape, x.dtype) for x in results),
+        in_specs=[vmem, vmem, vmem],
+        out_specs=(hbm, hbm, hbm),
+        scratch_shapes=[dma((3,))],
+    )(*results)
 
 
 def solution(mesh):

time: 153 us -> 149 us (0.974)
  the two profiles are of different devices: /device:TPU:1 before, /device:TPU:13 now
where the time goes in v2:
time: 149 us
  Pallas kernels  148 us (99%)
    pallas_call x1, Pallas kernels, local(): pl.pallas_call(fused_kernel, out_shape=(jax.ShapeDtypeStruct((HEIGHT, WID...  144 us
    pallas_call x1, Pallas kernels, local(): pl.pallas_call(write_kernel, out_shape=tuple((jax.ShapeDtypeStruct(x.shap...  3.63 us

profile of v2, /device:TPU:13, one launch (start us, length us, event | category | flops | bytes accessed | tf_op | source)
XLA Modules:
  0.0 148.5 jit_solution(10019797386835922331)
XLA Ops:
  0.6 144.3 %shard_map.76 = (bf16[32,128,128]{2,1,0:T(8,128)(2,1)}, bf16[32,128,128]{2,1,0:T(8,128)(2,1)}, f32[2,9,128,128]{3,2,1,0:T(8,128)}) custom-call(s32[2,8]{1,0:T(2,128)} %expert_ref.1, s32[256]{0:T(256)} %owner_ref.1, bf16[32,128,128]{2,1,0:T(8,128)(2,1)} %fields.1, bf16[32,128,128]{2,1,0:T(8,128)(2,1)} %cot.1, bf16[2,9,128,128]{3,2,1,0:T(8,128)(2,1)} %bank.1), custom_call_target="tpu_custom_call" | custom-call | tf_op jit(solution)/shard_map/pallas_call | solution.py:581
  144.9 3.6 %shard_map.77 = (bf16[32,128,128]{2,1,0:T(8,128)(2,1)}, bf16[32,128,128]{2,1,0:T(8,128)(2,1)}, f32[2,9,128,128]{3,2,1,0:T(8,128)}) custom-call(bf16[32,128,128]{2,1,0:T(8,128)(2,1)} %get-tuple-element.6.a, bf16[32,128,128]{2,1,0:T(8,128)(2,1)} %get-tuple-element.7.b, f32[2,9,128,128]{3,2,1,0:T(8,128)} %get-tuple-element.8.c), custom_call_target="tpu_custom_call" | custom-call | tf_op jit(solution)/shard_map/pallas_call | solution.py:650

commit v3 on v2

--- a/solution.py
+++ b/solution.py
@@ -20,19 +20,32 @@
 TILES = ROWS + 3
 EXT_ROWS = HEIGHT + 2
 EXT_COLS = WIDTH + 2 * BS
+PEERS = NLON - 1
 MESH = pl.DeviceIdType.MESH
 F32 = jnp.float32
 BF16 = jnp.bfloat16
 
 
+def turn(m):
+    return lax.rem(m + 1, RING)
+
+
+def torus_step(k):
+    p = lax.rem(k + 1, NLON)
+    i, j = p // RING, lax.rem(p, RING)
+    return lax.rem(i + 2 * j, RING), j
+
+
 def peer_lon(me, k):
     z, y = me // RING, lax.rem(me, RING)
-    return lax.rem(z + k // RING, RING) * RING + lax.rem(y + lax.rem(k, RING), RING)
+    dz, dy = torus_step(k)
+    return lax.rem(z + dz, RING) * RING + lax.rem(y + dy, RING)
 
 
 def source_lon(me, k):
     z, y = me // RING, lax.rem(me, RING)
-    return lax.rem(z + RING - k // RING, RING) * RING + lax.rem(y + RING - lax.rem(k, RING), RING)
+    dz, dy = torus_step(k)
+    return lax.rem(z + RING - dz, RING) * RING + lax.rem(y + RING - dy, RING)
 
 
 def greet(lat, lon, diagonal):
@@ -41,7 +54,7 @@
     def signal(device):
         pl.semaphore_signal(barrier, inc=1, device_id=device, device_id_type=MESH)
 
-    @pl.loop(1, NLON)
+    @pl.loop(0, PEERS)
     def _(k):
         signal((lat, peer_lon(lon, k)))
 
@@ -81,15 +94,15 @@
 
 def fused_kernel(
     expert_ref, owner_ref, fields, cot, bank,
-    outputs, result, bank_out,
-    home, local, slot_block, block_slot, ids, rank, order, final, canvas, ext,
+    outputs_hbm, result_hbm, bank_hbm,
+    outputs, result, bank_out, home, local, slot_block, block_slot, ids, rank, order, final, canvas, ext,
     col_stage, col_got, side_stage, sides, cot_in, patch_in, cot_stage, patch_stage, id_stage, got_cot, got_patch, got_id, kern,
     pad, taps, wide_cot, shift, total, running, out_stage, spread_stage, got_out, got_spread, block,
     pair_stage, got_pair, chip_stage, got_chip, row_in, col_in, corner_in,
     load_sem, cot_load, halo_send, halo_recv, bank_send, bank_recv, pass_send, pass_recv,
     cot_send, cot_recv, patch_send, patch_recv, id_send, id_recv,
     out_send, out_recv, spread_send, spread_recv, pair_sem, chip_send, chip_recv, edge_send, edge_recv,
-    own_sem,
+    own_sem, write_sem,
 ):
     lat, lon = lax.axis_index("lat"), lax.axis_index("lon")
     core = lax.rem(lat, 2)
@@ -122,8 +135,6 @@
     for b in range(BLK):
         c = home[b]
         block_slot[b] = 2 * c + jnp.where(slot_block[2 * c + 1] == b, 1, 0)
-    await_greetings(DIAGONAL)
-
     up, down = lax.rem(lat + NLAT - 1, NLAT), lax.rem(lat + 1, NLAT)
     left, right = lax.rem(lon + NLON - 1, NLON), lax.rem(lon + 1, NLON)
     top, bottom = pl.ds(0, 1), pl.ds(HEIGHT - 1, 1)
@@ -139,34 +150,6 @@
         (bottom, first, zero, high, (down, left)),
         (bottom, last, zero, low, (down, right)),
     )
-    halos = []
-    for i, (rows, cols, to_rows, to_cols, device) in enumerate(moves):
-        copy = remote(
-            fields.at[rows, cols], ext.at[to_rows, to_cols], halo_send.at[i], halo_recv.at[i], device
-        )
-        copy.start()
-        halos.append(copy)
-
-    def column(where):
-        return pl.ds(EXT_COLS + where, HEIGHT, stride=EXT_COLS)
-
-    outer_left, inner_left, inner_right, outer_right = BS - 1, BS, BS + WIDTH - 1, BS + WIDTH
-    load_fields.wait()
-
-    def widen(r):
-        canvas[pl.ds(pl.multiple_of(r * EXT_COLS, BS), EXT_COLS), :] = ext[r].astype(F32)
-
-    @pl.loop(1, HEIGHT + 1)
-    def _(r):
-        widen(r)
-
-    col_stage[0] = canvas[column(inner_left), :].astype(BF16)
-    col_stage[1] = canvas[column(inner_right), :].astype(BF16)
-    for i, device in enumerate(((lat, left), (lat, right))):
-        copy = remote(col_stage.at[i], col_got.at[i], halo_send.at[6 + i], halo_recv.at[6 + i], device)
-        copy.start()
-        halos.append(copy)
-
     def bank_copy(j):
         return remote(
             bank, kern.at[pl.ds(2 * lat, 2)], bank_send.at[j], bank_recv.at[j],
@@ -180,9 +163,6 @@
     share_bank = remote(
         bank, kern.at[pl.ds(2 * lat, 2)], pass_send.at[0], pass_recv.at[0], (other, lon)
     )
-    for j in range(1, RING):
-        bank_copy(j).start()
-    share_bank.start()
 
     def cot_copy(k, r):
         dst = peer_lon(lon, k)
@@ -224,6 +204,25 @@
     own_out = own(out_stage.at[own_slots], got_out.at[own_slots], 3)
     own_spread = own(spread_stage.at[own_slots], got_spread.at[own_slots], 4)
 
+    def stage_cot(k, r):
+        dst = peer_lon(lon, k)
+        cot_stage[dst, r] = cot_in[jnp.maximum(slot_block[2 * dst + r], 0)]
+
+    def column(where):
+        return pl.ds(EXT_COLS + where, HEIGHT, stride=EXT_COLS)
+
+    outer_left, inner_left, inner_right, outer_right = BS - 1, BS, BS + WIDTH - 1, BS + WIDTH
+    load_fields.wait()
+
+    def widen(r):
+        canvas[pl.ds(pl.multiple_of(r * EXT_COLS, BS), EXT_COLS), :] = ext[r].astype(F32)
+
+    @pl.loop(1, HEIGHT + 1)
+    def _(r):
+        widen(r)
+
+    col_stage[0] = canvas[column(inner_left), :].astype(BF16)
+    col_stage[1] = canvas[column(inner_right), :].astype(BF16)
     lane = lax.broadcasted_iota(jnp.int32, (1, C), 1)
 
     @pl.loop(0, NLON)
@@ -232,22 +231,44 @@
         named = [jnp.where(f < 0, NLON, local[jnp.maximum(f, 0)]) for f in found]
         id_stage[c] = jnp.where(lane == 0, named[0], named[1])
 
-    @pl.loop(1, NLON)
-    def _(k):
-        id_copy(k).start()
-
     @pl.loop(0, BLK)
     def _(b):
         load_cot(b).wait()
 
-    def stage_cot(k, r):
-        dst = peer_lon(lon, k)
-        cot_stage[dst, r] = cot_in[jnp.maximum(slot_block[2 * dst + r], 0)]
-
-    @pl.loop(1, NLON)
-    def _(k):
-        stage_cot(k, 0)
+    @pl.loop(0, NLON)
+    def _(k):
+        for r in range(CAP):
+            stage_cot(k, r)
+
+    own_cot.start()
+    own_id.start()
+    await_greetings(DIAGONAL)
+
+    @pl.loop(0, PEERS)
+    def _(k):
         cot_copy(k, 0).start()
+
+    halos = []
+    for i, (rows, cols, to_rows, to_cols, device) in enumerate(moves):
+        copy = remote(
+            fields.at[rows, cols], ext.at[to_rows, to_cols], halo_send.at[i], halo_recv.at[i], device
+        )
+        copy.start()
+        halos.append(copy)
+
+    for i, device in enumerate(((lat, left), (lat, right))):
+        copy = remote(col_stage.at[i], col_got.at[i], halo_send.at[6 + i], halo_recv.at[6 + i], device)
+        copy.start()
+        halos.append(copy)
+
+    for j in range(1, RING):
+        bank_copy(j).start()
+    share_bank.start()
+
+    @pl.loop(0, PEERS)
+    def _(k):
+        id_copy(k).start()
+        cot_copy(k, 1).start()
 
     for copy in halos:
         copy.wait()
@@ -279,27 +300,19 @@
         dst = peer_lon(lon, k)
         patch_stage[dst, r] = patch_in[jnp.maximum(slot_block[2 * dst + r], 0)]
 
-    @pl.loop(1, NLON)
+    @pl.loop(0, PEERS)
     def _(k):
         stage_patch(k, 0)
         patch_copy(k, 0).start()
 
-    @pl.loop(1, NLON)
-    def _(k):
-        stage_cot(k, 1)
-        cot_copy(k, 1).start()
-
-    @pl.loop(1, NLON)
+    @pl.loop(0, PEERS)
     def _(k):
         stage_patch(k, 1)
         patch_copy(k, 1).start()
 
     for r in range(CAP):
-        stage_cot(0, r)
-        stage_patch(0, r)
-    own_cot.start()
+        stage_patch(PEERS, r)
     own_patch.start()
-    own_id.start()
 
     load_bank.wait()
     for j in range(1, RING):
@@ -308,7 +321,7 @@
 
     own_id.wait()
 
-    @pl.loop(1, NLON)
+    @pl.loop(0, PEERS)
     def _(k):
         id_copy(k).wait()
 
@@ -391,22 +404,22 @@
         r, k = step // NLON, lax.rem(step, NLON)
         source = source_lon(lon, k)
 
-        @pl.when(k > 0)
+        @pl.when(k < PEERS)
         def _():
             cot_copy(k, r).wait_recv()
             patch_copy(k, r).wait_recv()
 
         convolve(2 * source + r, jnp.minimum(ids[source, 0, r], NLON - 1))
 
-        @pl.when(k > 0)
+        @pl.when(k < PEERS)
         def _():
             spread_copy(k, r).start()
 
-        @pl.when((k > 0) & (r == 0))
+        @pl.when((k < PEERS) & (r == 0))
         def _():
             out_copy(k, r).start()
 
-    @pl.loop(1, NLON)
+    @pl.loop(0, PEERS)
     def _(k):
         out_copy(k, 1).start()
 
@@ -463,7 +476,7 @@
 
     own_spread.wait()
 
-    @pl.loop(1, NLON)
+    @pl.loop(0, PEERS)
     def _(k):
         for r in range(CAP):
             spread_copy(k, r).wait_recv()
@@ -509,9 +522,14 @@
         for i in range(2):
             bank_out[i] += got_chip[back, i].astype(F32)
 
+    writes = [
+        pltpu.make_async_copy(x, y, write_sem.at[i])
+        for i, (x, y) in enumerate(((bank_out, bank_hbm), (outputs, outputs_hbm), (result, result_hbm)))
+    ]
+    writes[0].start()
     own_out.wait()
 
-    @pl.loop(1, NLON)
+    @pl.loop(0, PEERS)
     def _(k):
         for r in range(CAP):
             out_copy(k, r).wait_recv()
@@ -522,6 +540,8 @@
         outputs[
             pl.ds(pl.multiple_of(bi * BS, BS), BS), pl.ds(pl.multiple_of(bj * BS, BS), BS), :
         ] = got_out[block_slot[b]]
+
+    writes[1].start()
 
     def round_cells(i, col, count):
         start = pl.multiple_of((i + 1) * EXT_COLS + BS + col, BS)
@@ -554,7 +574,9 @@
         round_cells(i, 0, BS)
         round_cells(i, WIDTH - BS, BS)
 
-    @pl.loop(1, NLON)
+    writes[2].start()
+
+    @pl.loop(0, PEERS)
     def _(k):
         for r in range(CAP):
             cot_copy(k, r).wait_send()
@@ -562,10 +584,21 @@
             spread_copy(k, r).wait_send()
             out_copy(k, r).wait_send()
 
+    for copy in writes:
+        copy.wait()
+
 
 def write_kernel(a, b, c, a_out, b_out, c_out, sem):
-    pairs = ((a, a_out), (b, b_out), (c, c_out))
-    copies = [pltpu.make_async_copy(x, y, sem.at[i]) for i, (x, y) in enumerate(pairs)]
+    quarter = HEIGHT // 4
+    copies = []
+    for source, target in ((a, a_out), (b, b_out)):
+        for i in range(4):
+            part = pl.ds(i * quarter, quarter)
+            copies.append((source.at[part], target.at[part]))
+    for i in range(2):
+        for part in (pl.ds(0, 5), pl.ds(5, 4)):
+            copies.append((c.at[i, part], c_out.at[i, part]))
+    copies = [pltpu.make_async_copy(x, y, sem.at[i]) for i, (x, y) in enumerate(copies)]
     for copy in copies:
         copy.start()
     for copy in copies:
@@ -586,8 +619,11 @@
             jax.ShapeDtypeStruct((2, 9, C, C), F32),
         ),
         in_specs=[smem, smem, hbm, hbm, hbm],
-        out_specs=(vmem, vmem, vmem),
+        out_specs=(hbm, hbm, hbm),
         scratch_shapes=[
+            pltpu.VMEM((HEIGHT, WIDTH, C), BF16),
+            pltpu.VMEM((HEIGHT, WIDTH, C), BF16),
+            pltpu.VMEM((2, 9, C, C), F32),
             pltpu.SMEM((BLK,), jnp.int32),
             pltpu.SMEM((BLK,), jnp.int32),
             pltpu.SMEM((slots,), jnp.int32),
@@ -641,7 +677,7 @@
             dma((2,)),
             dma((RING,)), dma((RING,)),
             dma((8,)), dma((8,)),
-            dma((5,)),
+            dma((5,)), dma((3,)),
         ],
         compiler_params=pltpu.CompilerParams(
             collective_id=0, has_side_effects=True, vmem_limit_bytes=62 << 20
@@ -652,7 +688,7 @@
         out_shape=tuple(jax.ShapeDtypeStruct(x.shape, x.dtype) for x in results),
         in_specs=[vmem, vmem, vmem],
         out_specs=(hbm, hbm, hbm),
-        scratch_shapes=[dma((3,))],
+        scratch_shapes=[dma((12,))],
     )(*results)
 
 

time: 149 us -> 143 us (0.960)
  the two profiles are of different devices: /device:TPU:13 before, /device:TPU:37 now
where the time goes in v3:
time: 143 us
  Pallas kernels  142 us (99%)
    pallas_call x1, Pallas kernels, local(): pl.pallas_call(fused_kernel, out_shape=(jax.ShapeDtypeStruct((HEIGHT, WID...  138 us
    pallas_call x1, Pallas kernels, local(): pl.pallas_call(write_kernel, out_shape=tuple((jax.ShapeDtypeStruct(x.shap...  3.7 us

profile of v3, /device:TPU:37, one launch (start us, length us, event | category | flops | bytes accessed | tf_op | source)
XLA Modules:
  0.0 142.8 jit_solution(17104734833342888101)
XLA Ops:
  0.6 138.5 %shard_map.76 = (bf16[32,128,128]{2,1,0:T(8,128)(2,1)}, bf16[32,128,128]{2,1,0:T(8,128)(2,1)}, f32[2,9,128,128]{3,2,1,0:T(8,128)}) custom-call(s32[2,8]{1,0:T(2,128)} %expert_ref.1, s32[256]{0:T(256)} %owner_ref.1, bf16[32,128,128]{2,1,0:T(8,128)(2,1)} %fields.1, bf16[32,128,128]{2,1,0:T(8,128)(2,1)} %cot.1, bf16[2,9,128,128]{3,2,1,0:T(8,128)(2,1)} %bank.1), custom_call_target="tpu_custom_call" | custom-call | tf_op jit(solution)/shard_map/pallas_call | solution.py:614
  139.1 3.7 %shard_map.77 = (bf16[32,128,128]{2,1,0:T(8,128)(2,1)}, bf16[32,128,128]{2,1,0:T(8,128)(2,1)}, f32[2,9,128,128]{3,2,1,0:T(8,128)}) custom-call(bf16[32,128,128]{2,1,0:T(8,128)(2,1)} %get-tuple-element.6.a, bf16[32,128,128]{2,1,0:T(8,128)(2,1)} %get-tuple-element.7.b, f32[2,9,128,128]{3,2,1,0:T(8,128)} %get-tuple-element.8.c), custom_call_target="tpu_custom_call" | custom-call | tf_op jit(solution)/shard_map/pallas_call | solution.py:686

commit v4 on v3

--- a/solution.py
+++ b/solution.py
@@ -16,8 +16,9 @@
 HEIGHT = 32
 WIDTH = 128
 ROWS = BS + 2
-SIDE = 24
-TILES = ROWS + 3
+SIDE = ROWS
+CELLS = ROWS * BS
+PIECE = CELLS + 40
 EXT_ROWS = HEIGHT + 2
 EXT_COLS = WIDTH + 2 * BS
 PEERS = NLON - 1
@@ -121,6 +122,9 @@
     load_fields.start()
     load_bank = pltpu.make_async_copy(bank, kern.at[pl.ds(2 * lat, 2)], load_sem.at[1])
     load_bank.start()
+
+    def step_of(t):
+        return t + core * (PEERS - 1 - 2 * t)
 
     def load_cot(b):
         rows = pl.ds(pl.multiple_of((b // BLON) * BS, BS), BS)
@@ -245,7 +249,8 @@
     await_greetings(DIAGONAL)
 
     @pl.loop(0, PEERS)
-    def _(k):
+    def _(t):
+        k = step_of(t)
         cot_copy(k, 0).start()
 
     halos = []
@@ -266,7 +271,8 @@
     share_bank.start()
 
     @pl.loop(0, PEERS)
-    def _(k):
+    def _(t):
+        k = step_of(t)
         id_copy(k).start()
         cot_copy(k, 1).start()
 
@@ -290,23 +296,25 @@
     def _(b):
         row = pl.multiple_of((b // BLON) * BS, BS)
         col = pl.multiple_of((lax.rem(b, BLON) + 1) * BS, BS)
-        patch_in[b, pl.ds(0, ROWS)] = ext[pl.ds(row, ROWS), pl.ds(col, BS), :]
+        patch_in[b, pl.ds(0, CELLS)] = ext[pl.ds(row, ROWS), pl.ds(col, BS), :].reshape(CELLS, C)
         start = row * EXT_COLS + col
         sides[pl.ds(0, ROWS), :] = canvas[pl.ds(start - 1, ROWS, stride=EXT_COLS), :]
         sides[pl.ds(SIDE, ROWS), :] = canvas[pl.ds(start + BS, ROWS, stride=EXT_COLS), :]
-        patch_in[b, pl.ds(ROWS, 3)] = sides[...].astype(BF16).reshape(3, BS, C)
+        patch_in[b, pl.ds(CELLS, 40)] = sides[...].astype(BF16)
 
     def stage_patch(k, r):
         dst = peer_lon(lon, k)
         patch_stage[dst, r] = patch_in[jnp.maximum(slot_block[2 * dst + r], 0)]
 
     @pl.loop(0, PEERS)
-    def _(k):
+    def _(t):
+        k = step_of(t)
         stage_patch(k, 0)
         patch_copy(k, 0).start()
 
     @pl.loop(0, PEERS)
-    def _(k):
+    def _(t):
+        k = step_of(t)
         stage_patch(k, 1)
         patch_copy(k, 1).start()
 
@@ -364,10 +372,10 @@
         pass_copy(j).wait()
 
     def build_taps(slot):
-        pad[:, pl.ds(8, BS), :] = got_patch[slot, pl.ds(0, ROWS)].astype(F32)
-        both = got_patch[slot, pl.ds(ROWS, 3)].reshape(3 * BS, C).astype(F32)
-        pad[:, 7, :] = both[:ROWS]
-        pad[:, BS + 8, :] = both[SIDE:SIDE + ROWS]
+        pad[:, pl.ds(8, BS), :] = got_patch[slot, pl.ds(0, CELLS)].reshape(ROWS, BS, C).astype(F32)
+        sides[...] = got_patch[slot, pl.ds(CELLS, 40)].astype(F32)
+        pad[:, 7, :] = sides[pl.ds(0, ROWS), :]
+        pad[:, BS + 8, :] = sides[pl.ds(SIDE, ROWS), :]
         for b in range(3):
             taps[:, pl.ds(b * C, C)] = pad[:, pl.ds(7 + b, BS), :].reshape(ROWS * BS, C).astype(BF16)
 
@@ -391,17 +399,18 @@
         main = grid[:, C:2 * C].reshape(ROWS, BS, C)
         main += jnp.where(place == BS - 1, 0.0, shift[0, :, pl.ds(9, BS), :])
         main += jnp.where(place == 0, 0.0, shift[1, :, pl.ds(7, BS), :])
-        spread_stage[slot, pl.ds(0, ROWS)] = main.astype(BF16)
+        spread_stage[slot, pl.ds(0, CELLS)] = main.astype(BF16).reshape(CELLS, C)
         sides[pl.ds(0, ROWS), :] = shift[0, :, 8, :]
         sides[pl.ds(SIDE, ROWS), :] = shift[1, :, BS + 7, :]
-        spread_stage[slot, pl.ds(ROWS, 3)] = sides[...].astype(BF16).reshape(3, BS, C)
+        spread_stage[slot, pl.ds(CELLS, 40)] = sides[...].astype(BF16)
 
     own_cot.wait()
     own_patch.wait()
 
     @pl.loop(0, CAP * NLON)
     def _(step):
-        r, k = step // NLON, lax.rem(step, NLON)
+        r, t = step // NLON, lax.rem(step, NLON)
+        k = jnp.where(t < PEERS, step_of(t), t)
         source = source_lon(lon, k)
 
         @pl.when(k < PEERS)
@@ -420,7 +429,8 @@
             out_copy(k, r).start()
 
     @pl.loop(0, PEERS)
-    def _(k):
+    def _(t):
+        k = step_of(t)
         out_copy(k, 1).start()
 
     own_out.start()
@@ -489,10 +499,10 @@
 
         for i in range(ROWS):
             at = pl.ds(pl.multiple_of(base + i * EXT_COLS, BS), BS)
-            canvas[at, :] += block[i].astype(F32)
-        both = block[pl.ds(ROWS, 3)].reshape(3 * BS, C).astype(F32)
-        canvas[pl.ds(base - 1, ROWS, stride=EXT_COLS), :] += both[:ROWS]
-        canvas[pl.ds(base + BS, ROWS, stride=EXT_COLS), :] += both[SIDE:SIDE + ROWS]
+            canvas[at, :] += block[pl.ds(i * BS, BS)].astype(F32)
+        sides[...] = block[pl.ds(CELLS, 40)].astype(F32)
+        canvas[pl.ds(base - 1, ROWS, stride=EXT_COLS), :] += sides[pl.ds(0, ROWS), :]
+        canvas[pl.ds(base + BS, ROWS, stride=EXT_COLS), :] += sides[pl.ds(SIDE, ROWS), :]
 
     side_stage[0] = canvas[column(outer_left), :]
     side_stage[1] = canvas[column(outer_right), :]
@@ -637,14 +647,14 @@
             pltpu.VMEM((2, HEIGHT, C), BF16),
             pltpu.VMEM((2, HEIGHT, C), BF16),
             pltpu.VMEM((2, HEIGHT, C), F32),
-            pltpu.VMEM((3 * BS, C), F32),
+            pltpu.VMEM((40, C), F32),
             pltpu.VMEM((BLK, BS, BS, C), BF16),
-            pltpu.VMEM((BLK, TILES, BS, C), BF16),
+            pltpu.VMEM((BLK, PIECE, C), BF16),
             pltpu.VMEM((NLON, CAP, BS, BS, C), BF16),
-            pltpu.VMEM((NLON, CAP, TILES, BS, C), BF16),
+            pltpu.VMEM((NLON, CAP, PIECE, C), BF16),
             pltpu.VMEM((NLON, 1, C), jnp.int32),
             pltpu.VMEM((slots, BS, BS, C), BF16),
-            pltpu.VMEM((slots, TILES, BS, C), BF16),
+            pltpu.VMEM((slots, PIECE, C), BF16),
             pltpu.VMEM((NLON, 1, C), jnp.int32),
             pltpu.VMEM((NLON, 9, C, C), BF16),
             pltpu.VMEM((ROWS, 2 * BS, C), F32),
@@ -654,10 +664,10 @@
             pltpu.VMEM((9, C, C), F32),
             pltpu.VMEM((slots, 9, C, C), BF16),
             pltpu.VMEM((slots, BS, BS, C), BF16),
-            pltpu.VMEM((slots, TILES, BS, C), BF16),
+            pltpu.VMEM((slots, PIECE, C), BF16),
             pltpu.VMEM((slots, BS, BS, C), BF16),
-            pltpu.VMEM((slots, TILES, BS, C), BF16),
-            pltpu.VMEM((TILES, BS, C), BF16),
+            pltpu.VMEM((slots, PIECE, C), BF16),
+            pltpu.VMEM((PIECE, C), BF16),
             pltpu.VMEM((NLAT, 9, C, C), BF16),
             pltpu.VMEM((NLAT, 9, C, C), BF16),
             pltpu.VMEM((RING, 2, 9, C, C), BF16),

time: 143 us -> 132 us (0.923)
  the two profiles are of different devices: /device:TPU:37 before, /device:TPU:1 now
where the time goes in v4:
time: 132 us
  Pallas kernels  131 us (99%)
    pallas_call x1, Pallas kernels, local(): pl.pallas_call(fused_kernel, out_shape=(jax.ShapeDtypeStruct((HEIGHT, WID...  128 us
    pallas_call x1, Pallas kernels, local(): pl.pallas_call(write_kernel, out_shape=tuple((jax.ShapeDtypeStruct(x.shap...  3.7 us

profile of v4, /device:TPU:1, one launch (start us, length us, event | category | flops | bytes accessed | tf_op | source)
XLA Modules:
  0.0 132.0 jit_solution(4005595717798432776)
XLA Ops:
  0.6 127.6 %shard_map.76 = (bf16[32,128,128]{2,1,0:T(8,128)(2,1)}, bf16[32,128,128]{2,1,0:T(8,128)(2,1)}, f32[2,9,128,128]{3,2,1,0:T(8,128)}) custom-call(s32[2,8]{1,0:T(2,128)} %expert_ref.1, s32[256]{0:T(256)} %owner_ref.1, bf16[32,128,128]{2,1,0:T(8,128)(2,1)} %fields.1, bf16[32,128,128]{2,1,0:T(8,128)(2,1)} %cot.1, bf16[2,9,128,128]{3,2,1,0:T(8,128)(2,1)} %bank.1), custom_call_target="tpu_custom_call" | custom-call | tf_op jit(solution)/shard_map/pallas_call | solution.py:624
  128.3 3.7 %shard_map.77 = (bf16[32,128,128]{2,1,0:T(8,128)(2,1)}, bf16[32,128,128]{2,1,0:T(8,128)(2,1)}, f32[2,9,128,128]{3,2,1,0:T(8,128)}) custom-call(bf16[32,128,128]{2,1,0:T(8,128)(2,1)} %get-tuple-element.6.a, bf16[32,128,128]{2,1,0:T(8,128)(2,1)} %get-tuple-element.7.b, f32[2,9,128,128]{3,2,1,0:T(8,128)} %get-tuple-element.8.c), custom_call_target="tpu_custom_call" | custom-call | tf_op jit(solution)/shard_map/pallas_call | solution.py:696

commit v5 on v4

--- a/solution.py
+++ b/solution.py
@@ -34,7 +34,9 @@
 def torus_step(k):
     p = lax.rem(k + 1, NLON)
     i, j = p // RING, lax.rem(p, RING)
-    return lax.rem(i + 2 * j, RING), j
+    a, b = lax.rem(i + 2 * j, RING), j
+    swap = lax.rem(lax.axis_index("lat"), 2)
+    return a + swap * (b - a), b + swap * (a - b)
 
 
 def peer_lon(me, k):
@@ -122,9 +124,6 @@
     load_fields.start()
     load_bank = pltpu.make_async_copy(bank, kern.at[pl.ds(2 * lat, 2)], load_sem.at[1])
     load_bank.start()
-
-    def step_of(t):
-        return t + core * (PEERS - 1 - 2 * t)
 
     def load_cot(b):
         rows = pl.ds(pl.multiple_of((b // BLON) * BS, BS), BS)
@@ -249,8 +248,7 @@
     await_greetings(DIAGONAL)
 
     @pl.loop(0, PEERS)
-    def _(t):
-        k = step_of(t)
+    def _(k):
         cot_copy(k, 0).start()
 
     halos = []
@@ -271,8 +269,7 @@
     share_bank.start()
 
     @pl.loop(0, PEERS)
-    def _(t):
-        k = step_of(t)
+    def _(k):
         id_copy(k).start()
         cot_copy(k, 1).start()
 
@@ -307,14 +304,12 @@
         patch_stage[dst, r] = patch_in[jnp.maximum(slot_block[2 * dst + r], 0)]
 
     @pl.loop(0, PEERS)
-    def _(t):
-        k = step_of(t)
+    def _(k):
         stage_patch(k, 0)
         patch_copy(k, 0).start()
 
     @pl.loop(0, PEERS)
-    def _(t):
-        k = step_of(t)
+    def _(k):
         stage_patch(k, 1)
         patch_copy(k, 1).start()
 
@@ -409,8 +404,7 @@
 
     @pl.loop(0, CAP * NLON)
     def _(step):
-        r, t = step // NLON, lax.rem(step, NLON)
-        k = jnp.where(t < PEERS, step_of(t), t)
+        r, k = step // NLON, lax.rem(step, NLON)
         source = source_lon(lon, k)
 
         @pl.when(k < PEERS)
@@ -429,8 +423,7 @@
             out_copy(k, r).start()
 
     @pl.loop(0, PEERS)
-    def _(t):
-        k = step_of(t)
+    def _(k):
         out_copy(k, 1).start()
 
     own_out.start()

time: 132 us -> 129 us (0.977)
  Pallas kernels: 131 us -> 128 us
    pallas_call x1, Pallas kernels: 128 us -> 124 us  [local(): pl.pallas_call(fused_kernel, out_shape=(jax.ShapeDtypeStruct((HEIGHT, WID...]
where the time goes in v5:
time: 129 us; the launch traced here: 128 us
  Pallas kernels  128 us (99%)
    pallas_call x1, Pallas kernels, local(): pl.pallas_call(fused_kernel, out_shape=(jax.ShapeDtypeStruct((HEIGHT, WID...  124 us
    pallas_call x1, Pallas kernels, local(): pl.pallas_call(write_kernel, out_shape=tuple((jax.ShapeDtypeStruct(x.shap...  3.7 us

profile of v5, /device:TPU:1, one launch (start us, length us, event | category | flops | bytes accessed | tf_op | source)
XLA Modules:
  0.0 128.3 jit_solution(10554056264422425920)
XLA Ops:
  0.6 123.9 %shard_map.76 = (bf16[32,128,128]{2,1,0:T(8,128)(2,1)}, bf16[32,128,128]{2,1,0:T(8,128)(2,1)}, f32[2,9,128,128]{3,2,1,0:T(8,128)}) custom-call(s32[2,8]{1,0:T(2,128)} %expert_ref.1, s32[256]{0:T(256)} %owner_ref.1, bf16[32,128,128]{2,1,0:T(8,128)(2,1)} %fields.1, bf16[32,128,128]{2,1,0:T(8,128)(2,1)} %cot.1, bf16[2,9,128,128]{3,2,1,0:T(8,128)(2,1)} %bank.1), custom_call_target="tpu_custom_call" | custom-call | tf_op jit(solution)/shard_map/pallas_call | solution.py:617
  124.6 3.7 %shard_map.77 = (bf16[32,128,128]{2,1,0:T(8,128)(2,1)}, bf16[32,128,128]{2,1,0:T(8,128)(2,1)}, f32[2,9,128,128]{3,2,1,0:T(8,128)}) custom-call(bf16[32,128,128]{2,1,0:T(8,128)(2,1)} %get-tuple-element.6.a, bf16[32,128,128]{2,1,0:T(8,128)(2,1)} %get-tuple-element.7.b, f32[2,9,128,128]{3,2,1,0:T(8,128)} %get-tuple-element.8.c), custom_call_target="tpu_custom_call" | custom-call | tf_op jit(solution)/shard_map/pallas_call | solution.py:689

commit v6 on v5

--- a/solution.py
+++ b/solution.py
@@ -34,7 +34,7 @@
 def torus_step(k):
     p = lax.rem(k + 1, NLON)
     i, j = p // RING, lax.rem(p, RING)
-    a, b = lax.rem(i + 2 * j, RING), j
+    a, b = lax.rem(i + j, RING), j
     swap = lax.rem(lax.axis_index("lat"), 2)
     return a + swap * (b - a), b + swap * (a - b)
 

time: 129 us -> 136 us (1.054)
  Pallas kernels: 128 us -> 134 us
    pallas_call x1, Pallas kernels: 124 us -> 130 us  [local(): pl.pallas_call(fused_kernel, out_shape=(jax.ShapeDtypeStruct((HEIGHT, WID...]
where the time goes in v6:
time: 136 us; the launch traced here: 134 us
  Pallas kernels  134 us (99%)
    pallas_call x1, Pallas kernels, local(): pl.pallas_call(fused_kernel, out_shape=(jax.ShapeDtypeStruct((HEIGHT, WID...  130 us
    pallas_call x1, Pallas kernels, local(): pl.pallas_call(write_kernel, out_shape=tuple((jax.ShapeDtypeStruct(x.shap...  3.7 us

profile of v6, /device:TPU:1, one launch (start us, length us, event | category | flops | bytes accessed | tf_op | source)
XLA Modules:
  0.0 134.5 jit_solution(9820599289003640339)
XLA Ops:
  0.6 130.1 %shard_map.76 = (bf16[32,128,128]{2,1,0:T(8,128)(2,1)}, bf16[32,128,128]{2,1,0:T(8,128)(2,1)}, f32[2,9,128,128]{3,2,1,0:T(8,128)}) custom-call(s32[2,8]{1,0:T(2,128)} %expert_ref.1, s32[256]{0:T(256)} %owner_ref.1, bf16[32,128,128]{2,1,0:T(8,128)(2,1)} %fields.1, bf16[32,128,128]{2,1,0:T(8,128)(2,1)} %cot.1, bf16[2,9,128,128]{3,2,1,0:T(8,128)(2,1)} %bank.1), custom_call_target="tpu_custom_call" | custom-call | tf_op jit(solution)/shard_map/pallas_call | solution.py:617
  130.8 3.7 %shard_map.77 = (bf16[32,128,128]{2,1,0:T(8,128)(2,1)}, bf16[32,128,128]{2,1,0:T(8,128)(2,1)}, f32[2,9,128,128]{3,2,1,0:T(8,128)}) custom-call(bf16[32,128,128]{2,1,0:T(8,128)(2,1)} %get-tuple-element.6.a, bf16[32,128,128]{2,1,0:T(8,128)(2,1)} %get-tuple-element.7.b, f32[2,9,128,128]{3,2,1,0:T(8,128)} %get-tuple-element.8.c), custom_call_target="tpu_custom_call" | custom-call | tf_op jit(solution)/shard_map/pallas_call | solution.py:689

commit v7 on v5

--- a/solution.py
+++ b/solution.py
@@ -36,7 +36,8 @@
     i, j = p // RING, lax.rem(p, RING)
     a, b = lax.rem(i + 2 * j, RING), j
     swap = lax.rem(lax.axis_index("lat"), 2)
-    return a + swap * (b - a), b + swap * (a - b)
+    c, d = lax.rem(RING - a, RING), lax.rem(RING - b, RING)
+    return a + swap * (d - a), b + swap * (c - b)
 
 
 def peer_lon(me, k):

time: 129 us -> 134 us (1.039); the launches traced: 128 us -> 132 us
  Pallas kernels: 128 us -> 131 us
    pallas_call x1, Pallas kernels: 124 us -> 127 us  [local(): pl.pallas_call(fused_kernel, out_shape=(jax.ShapeDtypeStruct((HEIGHT, WID...]
where the time goes in v7:
time: 134 us; the launch traced here: 132 us
  Pallas kernels  131 us (98%)
    pallas_call x1, Pallas kernels, local(): pl.pallas_call(fused_kernel, out_shape=(jax.ShapeDtypeStruct((HEIGHT, WID...  127 us
    pallas_call x1, Pallas kernels, local(): pl.pallas_call(write_kernel, out_shape=tuple((jax.ShapeDtypeStruct(x.shap...  3.7 us

profile of v7, /device:TPU:1, one launch (start us, length us, event | category | flops | bytes accessed | tf_op | source)
XLA Modules:
  0.0 131.6 jit_solution(16571123111949955841)
XLA Ops:
  0.6 127.2 %shard_map.76 = (bf16[32,128,128]{2,1,0:T(8,128)(2,1)}, bf16[32,128,128]{2,1,0:T(8,128)(2,1)}, f32[2,9,128,128]{3,2,1,0:T(8,128)}) custom-call(s32[2,8]{1,0:T(2,128)} %expert_ref.1, s32[256]{0:T(256)} %owner_ref.1, bf16[32,128,128]{2,1,0:T(8,128)(2,1)} %fields.1, bf16[32,128,128]{2,1,0:T(8,128)(2,1)} %cot.1, bf16[2,9,128,128]{3,2,1,0:T(8,128)(2,1)} %bank.1), custom_call_target="tpu_custom_call" | custom-call | tf_op jit(solution)/shard_map/pallas_call | solution.py:618
  127.9 3.7 %shard_map.77 = (bf16[32,128,128]{2,1,0:T(8,128)(2,1)}, bf16[32,128,128]{2,1,0:T(8,128)(2,1)}, f32[2,9,128,128]{3,2,1,0:T(8,128)}) custom-call(bf16[32,128,128]{2,1,0:T(8,128)(2,1)} %get-tuple-element.6.a, bf16[32,128,128]{2,1,0:T(8,128)(2,1)} %get-tuple-element.7.b, f32[2,9,128,128]{3,2,1,0:T(8,128)} %get-tuple-element.8.c), custom_call_target="tpu_custom_call" | custom-call | tf_op jit(solution)/shard_map/pallas_call | solution.py:690
